TPU v7x, 32 devices: a whole 2x2x4 slice. The times are simulated.
32 devices in a mesh: dp: 8 (over z, x), ctx: 4 (over y, core).
Axes of the slice: x: 2, y: 2, z: 4, core: 2. Of those that a mesh axis runs over, the one named last changes fastest.
Arguments:
- tokens: bfloat16 [64, 1024, 576], P('dp', 'ctx'), may hold values from -6 to 6
- w_qkv: bfloat16 [552960], P(('dp', 'ctx')), may hold values from -0.25 to 0.25
- w_out: bfloat16 [331776], P(('dp', 'ctx')), may hold values from -1 to 1
- w_gate_up: bfloat16 [1769472], P(('dp', 'ctx')), may hold values from -0.25 to 0.25
- w_down: bfloat16 [884736], P(('dp', 'ctx')), may hold values from -0.15625 to 0.15625
- gains: bfloat16 [1152], P(('dp', 'ctx')), may hold values from 0.099609375 to 1.8984375
- cotangent: bfloat16 [64, 1024, 576], P('dp', 'ctx'), may hold values from -6 to 6
Outputs:
- output: bfloat16 [64, 1024, 576], P('dp', 'ctx')
- grad_input: bfloat16 [64, 1024, 576], P('dp', 'ctx')
- grad_qkv: float32 [552960], P(('dp', 'ctx'))
- grad_out: float32 [331776], P(('dp', 'ctx'))
- grad_gate_up: float32 [1769472], P(('dp', 'ctx'))
- grad_down: float32 [884736], P(('dp', 'ctx'))
- grad_gains: float32 [1152], P(('dp', 'ctx'))
All inputs are finite; a program needn't handle non-finite values.
Results may differ from a plain program's by a relative error of at most 0.014.
Values may be sent and summed in bfloat16 or wider, within the bound.
No kernel may reach another device: no remote copies, remote signals or barrier semaphores. Data moves between devices by JAX's collectives and lax.ppermute only.
A program may use at most 384 MiB of HBM per device.

v0:
```python
import math

import jax
import jax.numpy as jnp
from jax import lax
from jax.sharding import PartitionSpec as P

D = 576
HEADS = 9
KV_HEADS = 3
HEAD = 64
FF = 1536
QKVW = 960


EPSILON = 1e-05
THETA_BASE = 100000.0
NEG_FILL = -1e30


def angle_tables(positions, width):
    halves = jnp.arange(0, width, 2).astype(jnp.float32) / width
    inverse = jnp.exp(-math.log(THETA_BASE) * halves)
    angles = positions.astype(jnp.float32)[:, None] * inverse[None, :]
    angles = jnp.concatenate([angles, angles], axis=-1)
    return (jnp.cos(angles), jnp.sin(angles))


def rotate(values, cosine, sine):
    half = values.shape[-1] // 2
    turned = jnp.concatenate([-values[..., half:], values[..., :half]], axis=-1)
    return values * cosine + turned * sine


def unrotate(grads, cosine, sine):
    half = grads.shape[-1] // 2
    scaled = grads * sine
    turned = jnp.concatenate([scaled[..., half:], -scaled[..., :half]], axis=-1)
    return grads * cosine + turned


def fetch(part_qkv, part_out, part_gu, part_down, part_gains):
    result = (
        lax.all_gather(part_qkv, ("dp", "ctx"), axis=0, tiled=True),
        lax.all_gather(part_out, ("dp", "ctx"), axis=0, tiled=True),
        lax.all_gather(part_gu, ("dp", "ctx"), axis=0, tiled=True),
        lax.all_gather(part_down, ("dp", "ctx"), axis=0, tiled=True),
        lax.all_gather(part_gains, ("dp", "ctx"), axis=0, tiled=True),
    )
    return result


def settle(term_qkv, term_out, term_gu, term_down, term_gains):
    result = (
        lax.psum_scatter(term_qkv, ("dp", "ctx"), scatter_dimension=0, tiled=True),
        lax.psum_scatter(term_out, ("dp", "ctx"), scatter_dimension=0, tiled=True),
        lax.psum_scatter(term_gu, ("dp", "ctx"), scatter_dimension=0, tiled=True),
        lax.psum_scatter(term_down, ("dp", "ctx"), scatter_dimension=0, tiled=True),
        lax.psum_scatter(term_gains, ("dp", "ctx"), scatter_dimension=0, tiled=True),
    )
    return result


def attention_scores(queries, keys, allowed):
    raw = jnp.einsum("sqhgd,skhd->shgqk", queries, keys, preferred_element_type=jnp.float32) * 0.125
    return jnp.where(allowed, raw, NEG_FILL)


def local(tokens, w_qkv, w_out, w_gate_up, w_down, gains, cotangent):
    seqs_here = tokens.shape[0]
    span = tokens.shape[1]
    group = HEADS // KV_HEADS
    kv_width = KV_HEADS * HEAD
    row_count = seqs_here * span
    first = fetch(w_qkv, w_out, w_gate_up, w_down, gains)
    mat_qkv = first[0].reshape(D, QKVW)
    mat_out = first[1].reshape(D, D)
    mat_gu = first[2].reshape(D, 2 * FF)
    mat_down = first[3].reshape(FF, D)
    gain_one = first[4][:D].astype(jnp.float32)
    gain_two = first[4][D:].astype(jnp.float32)
    rows = tokens.reshape(row_count, D).astype(jnp.float32)
    inverse_one = lax.rsqrt(jnp.mean(rows * rows, axis=-1, keepdims=True) + EPSILON)
    normal_one = rows * inverse_one
    normed_one = (normal_one * gain_one).astype(jnp.bfloat16)
    projected = jnp.dot(normed_one, mat_qkv, preferred_element_type=jnp.float32)
    here = lax.axis_index("ctx") * span + jnp.arange(span)
    cos_here, sin_here = angle_tables(here, HEAD)
    cos_q = cos_here[None, :, None, :]
    sin_q = sin_here[None, :, None, :]
    queries = rotate(projected[:, :D].reshape(seqs_here, span, HEADS, HEAD), cos_q, sin_q)
    query_low = queries.astype(jnp.bfloat16).reshape(seqs_here, span, KV_HEADS, group, HEAD)
    key_low = rotate(
        projected[:, D : D + kv_width].reshape(seqs_here, span, KV_HEADS, HEAD), cos_q, sin_q
    ).astype(jnp.bfloat16)
    value_low = projected[:, D + kv_width :].astype(jnp.bfloat16)
    stacked = jnp.concatenate(
        [key_low.reshape(seqs_here, span, kv_width), value_low.reshape(seqs_here, span, kv_width)],
        axis=-1,
    )
    gathered = lax.all_gather(stacked, "ctx", axis=1, tiled=True)
    total_len = gathered.shape[1]
    key_all = gathered[..., :kv_width].reshape(seqs_here, total_len, KV_HEADS, HEAD)
    value_all = gathered[..., kv_width:].reshape(seqs_here, total_len, KV_HEADS, HEAD)
    places = jnp.arange(total_len)
    allowed = here[:, None] >= places[None, :]
    scores = attention_scores(query_low, key_all, allowed)
    highest = jnp.max(scores, axis=-1, keepdims=True)
    expo = jnp.exp(scores - highest)
    totals = jnp.sum(expo, axis=-1, keepdims=True)
    probs = expo / totals
    log_total = highest + jnp.log(totals)
    prob_low = probs.astype(jnp.bfloat16)
    mixed = jnp.einsum("shgqk,skhd->sqhgd", prob_low, value_all, preferred_element_type=jnp.float32)
    mixed_low = mixed.reshape(row_count, D).astype(jnp.bfloat16)
    residual = rows + jnp.dot(mixed_low, mat_out, preferred_element_type=jnp.float32)
    inverse_two = lax.rsqrt(jnp.mean(residual * residual, axis=-1, keepdims=True) + EPSILON)
    normal_two = residual * inverse_two
    normed_two = (normal_two * gain_two).astype(jnp.bfloat16)
    gate_up = jnp.dot(normed_two, mat_gu, preferred_element_type=jnp.float32)
    gate_part = gate_up[:, :FF]
    up_part = gate_up[:, FF:]
    sigmoid_gate = 1.0 / (1.0 + jnp.exp(-gate_part))
    activated = gate_part * sigmoid_gate
    product_low = (activated * up_part).astype(jnp.bfloat16)
    output = (residual + jnp.dot(product_low, mat_down, preferred_element_type=jnp.float32)).astype(
        jnp.bfloat16
    )
    second = fetch(w_qkv, w_out, w_gate_up, w_down, gains)
    back_qkv = second[0].reshape(D, QKVW)
    back_out = second[1].reshape(D, D)
    back_gu = second[2].reshape(D, 2 * FF)
    back_down = second[3].reshape(FF, D)
    grad_rows = cotangent.reshape(row_count, D)
    grad_down = jnp.dot(product_low.T, grad_rows, preferred_element_type=jnp.float32)
    grad_product = jnp.dot(grad_rows, back_down.T, preferred_element_type=jnp.float32)
    grad_gate = grad_product * up_part * sigmoid_gate * (1.0 + gate_part * (1.0 - sigmoid_gate))
    grad_up = grad_product * activated
    grad_gu_low = jnp.concatenate([grad_gate, grad_up], axis=-1).astype(jnp.bfloat16)
    grad_gate_up = jnp.dot(normed_two.T, grad_gu_low, preferred_element_type=jnp.float32)
    grad_normed_two = jnp.dot(grad_gu_low, back_gu.T, preferred_element_type=jnp.float32)
    grad_gain_two = jnp.sum(grad_normed_two * normal_two, axis=0)
    scaled_two = grad_normed_two * gain_two
    grad_residual = grad_rows.astype(jnp.float32) + inverse_two * (
        scaled_two - normal_two * jnp.mean(scaled_two * normal_two, axis=-1, keepdims=True)
    )
    grad_branch_low = grad_residual.astype(jnp.bfloat16)
    grad_out = jnp.dot(mixed_low.T, grad_branch_low, preferred_element_type=jnp.float32)
    grad_mixed_low = jnp.dot(
        grad_branch_low, back_out.T, preferred_element_type=jnp.float32
    ).astype(jnp.bfloat16)
    grad_mixed_low = grad_mixed_low.reshape(seqs_here, span, KV_HEADS, group, HEAD)
    scores_again = attention_scores(query_low, key_all, allowed)
    probs_again = jnp.exp(scores_again - log_total)
    prob_again_low = probs_again.astype(jnp.bfloat16)
    grad_probs = jnp.einsum(
        "sqhgd,skhd->shgqk", grad_mixed_low, value_all, preferred_element_type=jnp.float32
    )
    centre = jnp.sum(probs_again * grad_probs, axis=-1, keepdims=True)
    grad_scores_low = (probs_again * (grad_probs - centre)).astype(jnp.bfloat16)
    grad_queries = 0.125 * jnp.einsum(
        "shgqk,skhd->sqhgd", grad_scores_low, key_all, preferred_element_type=jnp.float32
    )
    grad_keys = 0.125 * jnp.einsum(
        "shgqk,sqhgd->skhd", grad_scores_low, query_low, preferred_element_type=jnp.float32
    )
    grad_values = jnp.einsum(
        "shgqk,sqhgd->skhd", prob_again_low, grad_mixed_low, preferred_element_type=jnp.float32
    )
    cos_all, sin_all = angle_tables(places, HEAD)
    grad_queries = unrotate(grad_queries.reshape(seqs_here, span, HEADS, HEAD), cos_q, sin_q)
    grad_keys = unrotate(grad_keys, cos_all[None, :, None, :], sin_all[None, :, None, :])
    kv_terms = jnp.concatenate(
        [
            grad_keys.reshape(seqs_here, total_len, kv_width),
            grad_values.reshape(seqs_here, total_len, kv_width),
        ],
        axis=-1,
    ).astype(jnp.bfloat16)
    kv_owned = lax.psum_scatter(kv_terms, "ctx", scatter_dimension=1, tiled=True).astype(
        jnp.float32
    )
    grad_proj_low = jnp.concatenate(
        [grad_queries.reshape(row_count, D), kv_owned.reshape(row_count, 2 * kv_width)], axis=-1
    ).astype(jnp.bfloat16)
    grad_qkv = jnp.dot(normed_one.T, grad_proj_low, preferred_element_type=jnp.float32)
    grad_normed_one = jnp.dot(grad_proj_low, back_qkv.T, preferred_element_type=jnp.float32)
    grad_gain_one = jnp.sum(grad_normed_one * normal_one, axis=0)
    scaled_one = grad_normed_one * gain_one
    grad_input = grad_residual + inverse_one * (
        scaled_one - normal_one * jnp.mean(scaled_one * normal_one, axis=-1, keepdims=True)
    )
    owned = settle(
        grad_qkv.reshape(-1),
        grad_out.reshape(-1),
        grad_gate_up.reshape(-1),
        grad_down.reshape(-1),
        jnp.concatenate([grad_gain_one, grad_gain_two]),
    )
    return (
        output.reshape(tokens.shape),
        grad_input.astype(jnp.bfloat16).reshape(tokens.shape),
        owned[0],
        owned[1],
        owned[2],
        owned[3],
        owned[4],
    )


def solution(mesh):
    in_specs = (
        P("dp", "ctx", None),
        P(("dp", "ctx")),
        P(("dp", "ctx")),
        P(("dp", "ctx")),
        P(("dp", "ctx")),
        P(("dp", "ctx")),
        P("dp", "ctx", None),
    )
    out_specs = (
        P("dp", "ctx", None),
        P("dp", "ctx", None),
        P(("dp", "ctx")),
        P(("dp", "ctx")),
        P(("dp", "ctx")),
        P(("dp", "ctx")),
        P(("dp", "ctx")),
    )
    return jax.shard_map(local, mesh=mesh, in_specs=in_specs, out_specs=out_specs, check_vma=False)
```

profile of v0, /device:TPU:0, one launch (start us, length us, event | category | flops | bytes accessed | tf_op | source)
XLA Modules:
  0.0 946.6 jit_solution(13876361599420750853)
XLA Ops:
  11.1 42.0 %all-reduce = bf16[1152]{0:T(1024)(128)(2,1)S(1)} all-reduce(bf16[1152]{0:T(1024)(128)(2,1)S(1)} %dynamic-update-slice), channel_id=1, replica_groups=mesh['dp'=8,'ctx'=4] {'dp','ctx'}, use_global_device_ids=true, to_apply=%add | all-reduce | flops 1152 | bytes 4608
  59.9 11.1 %all-gather.13.cloned.1.call-done = bf16[32,1,17280]{2,1,0:T(2,128)(2,1)} async-done(((bf16[1,1,17280]{2,1,0:T(2,128)(2,1)}), bf16[32,1,17280]{2,1,0:T(2,128)(2,1)}) %all-gather.13.cloned.1.call-update) | async-done | bytes 1105936 | tf_op jit(solution)/shard_map/all_gather | solution.py:44
  71.0 7.7 reduce.1
  81.1 4.7 fusion.55
  91.0 46.3 %all-gather.1 = bf16[32,1,10368]{2,1,0:T(2,128)(2,1)} all-gather(bf16[1,1,10368]{2,1,0:T(2,128)(2,1)S(1)} %reshape.317), channel_id=1, replica_groups=mesh['dp'=8,'ctx'=4] {'dp','ctx'}, dimensions={0}, use_global_device_ids=true | all-gather | bytes 684288 | tf_op jit(solution)/shard_map/all_gather | solution.py:45
  137.4 5.0 reduce.2
  144.1 3.4 copy.96
  148.0 2.8 copy.94
  161.7 4.7 reshape.298
  166.3 25.6 %all-gather.9.cloned.1.call-done = bf16[1769472]{0:T(1024)(128)(2,1)} async-done(((bf16[55296]{0:T(1024)(128)(2,1)}), bf16[1769472]{0:T(1024)(128)(2,1)}) %all-gather.9.cloned.1.call-update) | async-done | bytes 3538960 | tf_op jit(solution)/shard_map/all_gather | solution.py:46
  191.9 6.7 reshape.297
  198.6 41.3 %all-gather.7.cloned.1.call-done = bf16[8,1024,384]{1,0,2:T(8,128)(2,1)} async-done(((bf16[8,256,384]{1,0,2:T(8,128)(2,1)}), bf16[8,1024,384]{1,0,2:T(8,128)(2,1)}) %all-gather.7.cloned.1.call-update) | async-done | bytes 6291472 | tf_op jit(solution)/shard_map/all_gather | solution.py:101
  239.9 3.6 fusion.53
  245.2 3.5 copy.59
  248.7 27.1 %fusion.9 = (f32[8,3,3,256]{3,2,1,0:T(4,128)S(1)}, f32[8,3,1024,256,3]{3,2,4,1,0:T(8,128)}) fusion(pred[256,1024]{0,1:T(8,128)(4,1)S(1)} %iota_compare_fusion, bf16[8,1024,3,64,1]{1,3,4,2,0:T(8,128)(2,1)S(1)} %bitcast.178, bf16[8,256,3,3,64]{1,4,3,2,0:T(8,128)(2,1)S(1)} %fusion.18), kind=kOutput, calls=%fused_computation.14 | convolution fusion | flops 2472523776 | bytes 81338368 | tf_op jit(solution)/shard_map/sqhgd,skhd->shgqk/dot_general | solution.py:65
  275.9 24.8 %fusion.3 = f32[8,3,3,256]{3,2,1,0:T(4,128)} fusion(f32[8,3,3,256]{3,2,1,0:T(4,128)S(1)} %get-tuple-element.57, f32[8,3,1024,256,3]{3,2,4,1,0:T(8,128)} %get-tuple-element.58, pred[256,1024]{0,1:T(8,128)(4,1)S(1)} %iota_compare_fusion), kind=kLoop, calls=%fused_computation.9 | loop fusion | flops 75479040 | bytes 75907072 | tf_op jit(solution)/shard_map/reduce_sum | solution.py:110
  302.3 30.1 %convert_bitcast_fusion.1 = bf16[8,256,3,3,64]{1,4,3,2,0:T(8,128)(2,1)} fusion(bf16[8,1024,3,64,1]{1,3,4,2,0:T(8,128)(2,1)S(1)} %bitcast.194, f32[8,3,3,256]{3,2,1,0:T(4,128)} %fusion.3, f32[8,3,3,256]{3,2,1,0:T(4,128)S(1)} %get-tuple-element.57, f32[8,3,1024,256,3]{3,2,4,1,0:T(8,128)} %get-tuple-element.58, pred[256,1024]{0,1:T(8,128)(4,1)S(1)} %iota_compare_fusion), kind=kOutput, calls=%fused_computation.67 | convolution fusion | flops 2511470592 | bytes 81412096 | tf_op jit(solution)/shard_map/shgqk,skhd->sqhgd/dot_general | solution.py:114
  332.4 3.2 copy.65
  336.4 5.5 multiply_reduce_fusion.4
  341.9 14.0 %fusion.51 = f32[2048,3072]{1,0:T(8,128)} fusion(bf16[576,3072]{1,0:T(8,128)(2,1)S(1)} %copy-done.15, f32[2048,576]{0,1:T(8,128)S(1)} %get-tuple-element.60, f32[576]{0:T(1024)S(1)} %copy-done.34, f32[2048]{0:T(1024)S(1)} %add_rsqrt_fusion), kind=kOutput, calls=%fused_computation.114 | convolution fusion | flops 7251296256 | bytes 33433856 | tf_op jit(solution)/shard_map/dot_general | solution.py:120
  355.9 21.4 %multiply_convert_fusion.1 = (bf16[2048,1536]{1,0:T(8,128)(2,1)}, bf16[2048,1536]{1,0:T(8,128)(2,1)}, bf16[2048,1536]{1,0:T(8,128)(2,1)}) fusion(f32[2048,3072]{1,0:T(8,128)} %fusion.51, bf16[2048,576]{0,1:T(8,128)(2,1)} %bitcast.197, bf16[1536,576]{1,0:T(8,128)(2,1)} %reshape.298), kind=kOutput, calls=%fused_computation.17 | convolution fusion | flops 3671064576 | bytes 48168960 | tf_op jit(solution)/shard_map/dot_general | solution.py:136
  377.4 13.5 %multiply_reduce_fusion = (f32[576]{0:T(1024)}, f32[2048]{0:T(1024)S(1)}, f32[2048,576]{0,1:T(8,128)S(1)}) fusion(f32[2048,576]{0,1:T(8,128)} %copy-done, f32[2048]{0:T(1024)S(1)} %add_rsqrt_fusion, f32[576]{0:T(1024)S(1)} %copy-done.34, bf16[576,3072]{1,0:T(8,128)(2,1)} %reshape.297, bf16[2048,1536]{1,0:T(8,128)(2,1)} %get-tuple-element.37, ...), kind=kOutput, calls=%fused_computation.41 | convolution fusion | flops 7279998464 | bytes 25580032 | tf_op jit(solution)/shard_map/dot_general | solution.py:141
  396.9 30.5 %bitcast_convert_fusion = bf16[8,3,64,1024]{3,2,1,0:T(8,128)(2,1)} fusion(f32[8,3,3,256]{3,2,1,0:T(4,128)S(1)} %copy-done.26, f32[8,3,1024,256,3]{3,2,4,1,0:T(8,128)} %get-tuple-element.58, pred[256,1024]{0,1:T(8,128)(4,1)S(1)} %iota_compare_fusion, bf16[8,256,3,3,64]{1,0,4,3,2:T(8,128)(2,1)S(1)} %bitcast.203), kind=kOutput, calls=%fused_computation.29 | convolution fusion | flops 2492989440 | bytes 81338368 | tf_op jit(solution)/shard_map/shgqk,sqhgd->skhd/dot_general | solution.py:167
  427.4 57.9 %fusion = (f32[8,3,3,256]{3,2,1,0:T(4,128)}, f32[8,3,1024,256,3]{3,2,4,1,0:T(8,128)}) fusion(f32[8,3,3,256]{3,2,1,0:T(4,128)S(1)} %copy-done.26, f32[8,3,1024,256,3]{3,2,4,1,0:T(8,128)} %get-tuple-element.58, pred[256,1024]{0,1:T(8,128)(4,1)S(1)} %iota_compare_fusion, bf16[8,1024,3,64,1]{1,3,4,2,0:T(8,128)(2,1)S(1)} %bitcast.195, ...), kind=kOutput, calls=%fused_computation.2 | convolution fusion | flops 2510272512 | bytes 156909568 | tf_op jit(solution)/shard_map/sqhgd,skhd->shgqk/dot_general | solution.py:156
  485.3 6.2 copy.77
  491.5 59.9 %fusion.2 = bf16[8,3,3,256,1024]{3,4,2,1,0:T(8,128)(2,1)} fusion(f32[8,3,1024,256,3]{3,2,4,1,0:T(8,128)} %get-tuple-element.63, f32[8,3,3,256]{3,2,1,0:T(4,128)S(1)} %copy-done.27, f32[8,3,3,256]{3,2,1,0:T(4,128)S(1)} %copy-done.26, f32[8,3,1024,256,3]{3,2,4,1,0:T(8,128)} %get-tuple-element.58, pred[256,1024]{0,1:T(8,128)(4,1)S(1)} %iota_compare_fusion), kind=kLoop, calls=%fused_computation.4 | loop fusion | flops 113246208 | bytes 189153280 | tf_op jit(solution)/shard_map/convert_element_type | solution.py:160
  551.4 19.7 %bitcast_multiply_fusion.1 = (f32[8,1024,3,64]{1,3,2,0:T(8,128)S(1)}, f32[8,3,64,1024,1]{3,2,4,1,0:T(8,128)}) fusion(f32[1024,64]{0,1:T(8,128)S(1)} %copy-done.6, bf16[8,256,3,3,64]{1,4,3,2,0:T(8,128)(2,1)} %copy-done.5, bf16[8,3,3,256,1024]{3,4,2,1,0:T(8,128)(2,1)} %fusion.2), kind=kOutput, calls=%fused_computation.30 | convolution fusion | flops 2417491968 | bytes 52953088 | tf_op jit(solution)/shard_map/shgqk,sqhgd->skhd/dot_general | solution.py:164
  573.4 5.5 fusion.13
  578.9 4.1 copy.76
  583.1 8.4 pad_maximum_fusion.3
  592.8 4.4 copy.106
  597.2 8.9 fusion.56
  606.1 5.3 reshape.311
  611.4 13.1 %fusion.19 = f32[72,24,8,128]{3,2,1,0:T(8,128)S(1)} fusion(bf16[2048,1536]{1,0:T(8,128)(2,1)} %get-tuple-element.37, bf16[2048,1536]{1,0:T(8,128)(2,1)} %get-tuple-element.36, f32[2048,576]{0,1:T(8,128)} %copy-done, f32[576]{0:T(1024)S(1)} %copy-done.35, f32[2048]{0:T(1024)S(1)} %copy-done.31), kind=kOutput, calls=%fused_computation.56 | convolution fusion | flops 7276462080 | bytes 24389888 | tf_op jit(solution)/shard_map/dot_general | solution.py:140
  624.4 4.5 copy.108
  628.9 5.7 fusion.32
  634.5 2.8 reshape.309
  637.4 18.0 %broadcast_multiply_fusion = f32[8,3,64,3,256]{4,2,3,1,0:T(8,128)} fusion(bf16[8,1024,3,64,1]{1,3,4,2,0:T(8,128)(2,1)S(1)} %bitcast.179, bf16[8,3,3,256,1024]{3,4,2,1,0:T(8,128)(2,1)} %fusion.2), kind=kOutput, calls=%fused_computation.65 | convolution fusion | flops 2417098752 | bytes 45613056 | tf_op jit(solution)/shard_map/shgqk,skhd->sqhgd/dot_general | solution.py:161
  655.4 5.2 copy_multiply_fusion
  663.6 2.7 copy.71
  668.6 2.7 add_convert_fusion.1
  671.3 2.8 copy.78
  674.1 6.2 fusion.22
  684.3 8.2 add_convert_fusion.2
  695.5 4.5 multiply_reduce_fusion.1
  700.0 4.3 add_convert_fusion
  705.9 41.3 %all-reduce.5 = f32[1152]{0:T(1024)S(1)} all-reduce(f32[1152]{0:T(1024)S(1)} %pad_maximum_fusion.14), channel_id=7, replica_groups=mesh['dp'=8,'ctx'=4] {'dp','ctx'}, use_global_device_ids=true, to_apply=%region_14.15.clone | all-reduce | flops 1152 | bytes 9216
  747.8 185.4 %all-reduce.9.cloned.1.call-done = (f32[552960]{0:T(1024)}, f32[331776]{0:T(1024)}, f32[1769472]{0:T(1024)}, f32[884736]{0:T(1024)}) async-done(((f32[552960]{0:T(1024)}, f32[331776]{0:T(1024)}, f32[1769472]{0:T(1024)}, f32[884736]{0:T(1024)}), (f32[552960]{0:T(1024)}, f32[331776]{0:T(1024)}, f32[1769472]{0:T(1024)}, f32[884736]{0:T(1024)})) %all-reduce.9.cloned.1.call-update) | async-done | bytes 14155792
  (165 shorter events, 65.4 us)
Async XLA Ops:
  7.2 63.9 %all-gather.13.cloned.1.call-start = ((), (), s32[]{:S(2)}) async-start(), calls=%async_computation.5 | async-start | bytes 2280960 | tf_op jit(solution)/shard_map/all_gather | solution.py:44
  8.7 153.0 %all-gather.11.cloned.1.call-start = ((), (), s32[]{:S(2)}) async-start(), calls=%async_computation.3 | async-start | bytes 1824768 | tf_op jit(solution)/shard_map/all_gather | solution.py:47
  9.4 182.5 %all-gather.9.cloned.1.call-start = ((), (), s32[]{:S(2)}) async-start(), calls=%async_computation.2 | async-start | bytes 3649536 | tf_op jit(solution)/shard_map/all_gather | solution.py:46
  10.2 229.8 %all-gather.7.cloned.1.call-start = ((), (), s32[]{:S(2)}) async-start(), calls=%async_computation.1 | async-start | bytes 7864320 | tf_op jit(solution)/shard_map/all_gather | solution.py:101
  53.8 2.8 copy-start.28
  59.9 99.6 %copy-start.22 = (f32[256,64]{0,1:T(8,128)}, f32[256,64]{0,1:T(8,128)S(1)}, u32[]{:S(2)}) copy-start(f32[256,64]{0,1:T(8,128)S(1)} %get-tuple-element.52) | copy-start | bytes 196612
  85.8 3.1 copy-start.7
  86.3 2.9 copy-start.24
  89.2 1.8 copy-start.33
  90.9 580.4 %reduce-scatter.2.cloned.1.call-start = ((), (), s32[]{:S(2)}) async-start(), calls=%async_computation.4 | async-start | bytes 7864320 | tf_op jit(solution)/shard_map/reduce_scatter | solution.py:180
  91.0 56.5 %copy-start.4 = (bf16[8,256,576]{1,2,0:T(8,128)(2,1)S(1)}, bf16[8,256,576]{1,2,0:T(8,128)(2,1)}, u32[]{:S(2)}) copy-start(bf16[8,256,576]{1,2,0:T(8,128)(2,1)} %param.7) | copy-start | bytes 7077892
  152.9 2.3 slice-start.4
  161.6 87.1 %copy-start.5 = (bf16[8,256,3,3,64]{1,4,3,2,0:T(8,128)(2,1)}, bf16[8,256,3,3,64]{1,4,3,2,0:T(8,128)(2,1)S(1)}, u32[]{:S(2)}) copy-start(bf16[8,256,3,3,64]{1,4,3,2,0:T(8,128)(2,1)S(1)} %fusion.18) | copy-start | bytes 7077892
  245.2 30.7 %copy-start.2 = (bf16[8,1024,192]{1,2,0:T(8,128)(2,1)}, bf16[8,1024,192]{1,2,0:T(8,128)(2,1)S(1)}, u32[]{:S(2)}) copy-start(bf16[8,1024,192]{1,2,0:T(8,128)(2,1)S(1)} %copy.60) | copy-start | bytes 9437188
  275.9 26.4 %copy-start.11 = (bf16[8,1024,192]{1,2,0:T(8,128)(2,1)S(1)}, bf16[8,1024,192]{1,2,0:T(8,128)(2,1)}, u32[]{:S(2)}) copy-start(bf16[8,1024,192]{1,2,0:T(8,128)(2,1)} %copy.59) | copy-start | bytes 9437188
  332.4 4.0 copy-start.16
  336.3 5.5 copy-start.9
  336.4 5.6 copy-start.15
  336.4 5.6 copy-start.34
  341.9 14.0 %copy-start = (f32[2048,576]{0,1:T(8,128)}, f32[2048,576]{0,1:T(8,128)S(1)}, u32[]{:S(2)}) copy-start(f32[2048,576]{0,1:T(8,128)S(1)} %get-tuple-element.60) | copy-start | bytes 14155780
  341.9 48.9 %copy-start.30 = (f32[2048]{0:T(1024)}, f32[2048]{0:T(1024)S(1)}, u32[]{:S(2)}) copy-start(f32[2048]{0:T(1024)S(1)} %add_rsqrt_fusion) | copy-start | bytes 24580
  377.4 13.5 %copy-start.1 = (f32[2048,576]{0,1:T(8,128)S(1)}, f32[2048,576]{0,1:T(8,128)}, u32[]{:S(2)}) copy-start(f32[2048,576]{0,1:T(8,128)} %copy-done) | copy-start | bytes 14155780
  377.4 13.5 %copy-start.12 = (bf16[8,72,8,256]{3,2,0,1:T(8,128)(2,1)S(1)}, bf16[8,72,8,256]{3,2,0,1:T(8,128)(2,1)}, u32[]{:S(2)}) copy-start(bf16[8,72,8,256]{3,2,0,1:T(8,128)(2,1)} %copy.96) | copy-start | bytes 7077892
  390.9 1.6 copy-start.17
  392.5 2.2 copy-start.8
  394.7 2.2 copy-start.26
  395.5 1.4 copy-start.14
  485.3 6.2 copy-start.27
  491.5 59.9 %copy-start.6 = (f32[1024,64]{0,1:T(8,128)S(1)}, f32[1024,64]{0,1:T(8,128)}, u32[]{:S(2)}) copy-start(f32[1024,64]{0,1:T(8,128)} %get-tuple-element.50) | copy-start | bytes 786436
  571.1 2.4 copy-start.21
  591.5 341.8 %all-reduce.9.cloned.1.call-start = ((), (), s32[]{:S(2)}) async-start(), calls=%async_computation.6 | async-start | bytes 28311552
  592.8 4.4 copy-start.13
  606.1 5.3 copy-start.31
  606.1 5.3 copy-start.35
  624.4 4.5 copy-start.10
  628.9 8.5 copy-start.3
  637.4 18.1 %copy-start.23 = (f32[256,64]{0,1:T(8,128)S(1)}, f32[256,64]{0,1:T(8,128)}, u32[]{:S(2)}) copy-start(f32[256,64]{0,1:T(8,128)} %copy-done.22) | copy-start | bytes 196612
  660.9 2.6 slice-start.2
  661.3 2.3 slice-start.3
  663.6 5.0 slice-start.5
  666.4 2.3 slice-start.6
  668.6 5.4 copy-start.29
  682.7 1.5 copy-start.19
  682.7 11.3 %slice-start = ((s8[4718592]{0:T(1024)(128)(4,1)}), s8[524288]{0:T(1024)(128)(4,1)S(1)}, s32[]{:S(2)}) async-start(s8[4718592]{0:T(1024)(128)(4,1)} %bitcast.168), calls=%async_computation.7 | async-start | bytes 1048576
  684.3 9.8 %slice-start.1 = ((s8[4718592]{0:T(1024)(128)(4,1)}), s8[4194304]{0:T(1024)(128)(4,1)S(1)}, s32[]{:S(2)}) async-start(s8[4718592]{0:T(1024)(128)(4,1)} %bitcast.168), calls=%async_computation.8 | async-start | bytes 8388608
  692.5 2.6 copy-start.18
  692.5 3.0 copy-start.20
  704.3 1.6 copy-start.36
  (2 other events, 1.6 us)
Sparse Core Ops, SparseCore 0:
  11.4 59.5 all-gather.12
  73.8 55.6 all-gather.10
  132.5 59.3 all-gather.8
  193.9 46.0 all-gather.6
  591.6 58.3 reduce-scatter.1
  682.9 250.3 all-reduce.8
where the time goes:
time: 955 us; the launch traced here: 947 us
  matrix products  291 us (30%)
  waiting for transfers between devices  265 us (28%)
  other arithmetic  143 us (15%)
  blocking collectives  130 us (14%)
  local copies, waits for them, and re-layouts  103 us (11%)
  between operations  15.1 us (2%)
    unnamed x7, waiting for transfers between devices  187 us
    unnamed x2, blocking collectives  83.4 us
    convert_element_type x1, other arithmetic, local(): grad_scores_low = (probs_again * (grad_probs - centre)).astype(jnp.bfloat16)  59.9 us
    dot_general x1, matrix products, local(): jnp.einsum('sqhgd,skhd->shgqk', grad_mixed_low, value_all, preferred_elem...  57.9 us
    all_gather x1, blocking collectives, fetch(): lax.all_gather(part_out, ('dp', 'ctx'), axis=0, tiled=True)  46.3 us
    all_gather x1, waiting for transfers between devices, local(): gathered = lax.all_gather(stacked, 'ctx', axis=1, tiled=True)  41.3 us
    unnamed x105, local copies, waits for them, and re-layouts  34.6 us
    dot_general x1, matrix products, local(): jnp.einsum('shgqk,sqhgd->skhd', prob_again_low, grad_mixed_low, preferred...  30.5 us
  transfers between devices with their start and end apart: 6, of which 4 were waited for; matrix products, arithmetic and copies ran while one was open for 17% of the time, Pallas kernels for 0%

commit v1 on v0

v1 whole, which is shorter than its diff:
```python
import math

import jax
import jax.numpy as jnp
from jax import lax
from jax.experimental import pallas as pl
from jax.experimental.pallas import tpu as pltpu
from jax.sharding import PartitionSpec as P

D = 576
HEADS = 9
KV_HEADS = 3
HEAD = 64
FF = 1536
QKVW = 960
KV0 = D
V0 = D + KV_HEADS * HEAD
HALF = HEAD // 2
TILE = 256

EPSILON = 1e-05
THETA_BASE = 100000.0
NEG_FILL = -1e30
BF = jnp.bfloat16
F32 = jnp.float32


def nn(a, b):
    return lax.dot_general(a, b, (((1,), (0,)), ((), ())), preferred_element_type=F32)


def nt(a, b):
    return lax.dot_general(a, b, (((1,), (1,)), ((), ())), preferred_element_type=F32)


def eye(size):
    r = lax.broadcasted_iota(jnp.int32, (size, size), 0)
    c = lax.broadcasted_iota(jnp.int32, (size, size), 1)
    return jnp.where(r == c, 1.0, 0.0).astype(BF)


def col_chunks(width, step=128):
    return [(c, min(step, width - c)) for c in range(0, width, step)]


def flip(rows):
    parts = [nt(eye(w), rows[:, c : c + w]).astype(BF) for c, w in col_chunks(rows.shape[1])]
    return jnp.concatenate(parts, axis=0)


def unflip(cols):
    return nt(eye(cols.shape[1]), cols).astype(BF)


def inverse_rms(cols):
    return lax.rsqrt(jnp.sum(cols * cols, axis=0, keepdims=True) * (1.0 / D) + EPSILON)


def rotary_tables(length):
    halves = jnp.arange(0, HEAD, 2).astype(F32) / HEAD
    inverse = jnp.exp(-math.log(THETA_BASE) * halves)
    angles = inverse[:, None] * jnp.arange(length).astype(F32)[None, :]
    return jnp.cos(angles), jnp.sin(angles)


def tri_mask(size):
    key = lax.broadcasted_iota(jnp.int32, (size, size), 0)
    query = lax.broadcasted_iota(jnp.int32, (size, size), 1)
    return key <= query


def forward_kernel(me_ref, x_ref, wt_ref, gain_ref, cos_ref, sin_ref, xt_ref, qkv_ref, o_ref, lse_ref, krow):
    slices, _, span, _ = x_ref.shape
    length = slices * span
    me = me_ref[0]
    for k in range(slices):
        at = pl.multiple_of((me ^ k) * span, span)
        xt_ref[0, :, pl.ds(at, span)] = flip(x_ref[k, 0])
    gain = gain_ref[...]
    wt = wt_ref[...]
    for t in range(0, length, TILE):
        x = xt_ref[0, :, t : t + TILE].astype(F32)
        normed = (x * inverse_rms(x) * gain).astype(BF)
        proj = nn(wt, normed)
        cos = cos_ref[:, t : t + TILE]
        sin = sin_ref[:, t : t + TILE]
        for j in range(HEADS + KV_HEADS):
            u1 = proj[j * HEAD : j * HEAD + HALF]
            u2 = proj[j * HEAD + HALF : (j + 1) * HEAD]
            r1 = (u1 * cos - u2 * sin).astype(BF)
            r2 = (u2 * cos + u1 * sin).astype(BF)
            if j < HEADS:
                r1 = r1 * jnp.asarray(0.125, BF)
                r2 = r2 * jnp.asarray(0.125, BF)
            qkv_ref[0, j * HEAD : j * HEAD + HALF, t : t + TILE] = r1
            qkv_ref[0, j * HEAD + HALF : (j + 1) * HEAD, t : t + TILE] = r2
        qkv_ref[0, V0:, t : t + TILE] = proj[V0:].astype(BF)
        for j in range(KV_HEADS):
            krow[j, t : t + TILE, :] = unflip(qkv_ref[0, KV0 + j * HEAD : KV0 + (j + 1) * HEAD, t : t + TILE])

    keep = tri_mask(TILE)

    def head(h, carry):
        kv = h // (HEADS // KV_HEADS)
        rows = pl.ds(pl.multiple_of(h * HEAD, HEAD), HEAD)
        vrows = pl.ds(pl.multiple_of(V0 + kv * HEAD, HEAD), HEAD)
        for t in range(0, length, TILE):
            cols = slice(t, t + TILE)
            q = qkv_ref[0, rows, cols]
            last = jnp.where(keep, nn(krow[kv, cols, :], q), NEG_FILL)
            top = jnp.max(last, axis=0, keepdims=True)
            if t:
                before = nn(krow[kv, 0:t, :], q)
                top = jnp.maximum(top, jnp.max(before, axis=0, keepdims=True))
            e = jnp.exp(last - top)
            total = jnp.sum(e, axis=0, keepdims=True)
            acc = nn(qkv_ref[0, vrows, cols], e.astype(BF))
            if t:
                e = jnp.exp(before - top)
                total = total + jnp.sum(e, axis=0, keepdims=True)
                acc = acc + nn(qkv_ref[0, vrows, 0:t], e.astype(BF))
            o_ref[0, rows, cols] = (acc * (1.0 / total)).astype(BF)
            lse_ref[0, pl.ds(h, 1), cols] = top + jnp.log(total)
        return carry

    lax.fori_loop(0, HEADS, head, 0)


def middle_kernel(
    me_ref, xt_ref, o_ref, dy_ref, wo_ref, wgu_ref, wd_ref, gain_ref,
    out_ref, dr_ref, do_ref, delta_ref, gout_ref, ggu_ref, gdown_ref, gg_ref,
    wot, wgut, wdt, aout, agu, adown,
):
    step = pl.program_id(0) * pl.num_programs(1) + pl.program_id(1)
    last = pl.num_programs(0) * pl.num_programs(1) - 1

    @pl.when(step == 0)
    def _():
        for c in range(0, 2 * FF, TILE):
            wgut[c : c + TILE, :] = nt(eye(TILE), wgu_ref[:, c : c + TILE]).astype(BF)
        for c, w in col_chunks(D):
            wdt[c : c + w, :] = nt(eye(w), wd_ref[:, c : c + w]).astype(BF)
            wot[c : c + w, :] = nt(eye(w), wo_ref[:, c : c + w]).astype(BF)
        aout[...] = jnp.zeros_like(aout)
        agu[...] = jnp.zeros_like(agu)
        adown[...] = jnp.zeros_like(adown)
        gg_ref[...] = jnp.zeros_like(gg_ref)

    gain = gain_ref[...]
    o = o_ref[0]
    r = xt_ref[0].astype(F32) + nn(wot[...], o)
    inv = inverse_rms(r)
    n = r * inv
    h = (n * gain).astype(BF)
    a = nn(wgut[0:FF, :], h)
    u = nn(wgut[FF:, :], h)
    sg = 1.0 / (1.0 + jnp.exp(-a))
    act = a * sg
    m = (act * u).astype(BF)
    out_ref[0, 0] = unflip((r + nn(wdt[...], m)).astype(BF))
    dy = dy_ref[0, 0]
    dyt = flip(dy)
    adown[...] += nn(m, dy)
    dm = nn(wd_ref[...], dyt)
    da = (dm * u * sg * (1.0 + a * (1.0 - sg))).astype(BF)
    du = (dm * act).astype(BF)
    agu[:, 0:FF] += nt(h, da)
    agu[:, FF:] += nt(h, du)
    dh = nn(wgu_ref[:, 0:FF], da) + nn(wgu_ref[:, FF:], du)
    dhn = dh * n
    part = dhn[:, 0:128]
    for c in range(128, dhn.shape[1], 128):
        part = part + dhn[:, c : c + 128]
    gg_ref[...] += part
    e = dh * gain
    dr = dyt.astype(F32) + inv * (e - n * (jnp.sum(e * n, axis=0, keepdims=True) * (1.0 / D)))
    dr_ref[0] = dr
    db = dr.astype(BF)
    aout[...] += nt(o, db)
    do = nn(wo_ref[...], db).astype(BF)
    do_ref[0] = do
    prod = do.astype(F32) * o.astype(F32)
    for j in range(HEADS):
        delta_ref[0, j : j + 1, :] = jnp.sum(prod[j * HEAD : (j + 1) * HEAD], axis=0, keepdims=True)

    @pl.when(step == last)
    def _():
        gout_ref[...] = aout[...].astype(BF)
        ggu_ref[...] = agu[...].astype(BF)
        gdown_ref[...] = adown[...].astype(BF)


def backward_kernel(
    me_ref, xt_ref, qkv_ref, do_ref, lse_ref, delta_ref, dr_ref, w_ref, gain_ref, cos_ref, sin_ref,
    gin_ref, gqkv_ref, gg_ref,
    krow, vrow, grads, acc,
):
    slices, _, span, _ = gin_ref.shape
    length = slices * span
    me = me_ref[0]

    @pl.when(pl.program_id(0) == 0)
    def _():
        acc[...] = jnp.zeros_like(acc)
        gg_ref[...] = jnp.zeros_like(gg_ref)

    grads[...] = jnp.zeros_like(grads)
    for t in range(0, length, TILE):
        for j in range(KV_HEADS):
            krow[j, t : t + TILE, :] = unflip(qkv_ref[0, KV0 + j * HEAD : KV0 + (j + 1) * HEAD, t : t + TILE])
            vrow[j, t : t + TILE, :] = unflip(qkv_ref[0, V0 + j * HEAD : V0 + (j + 1) * HEAD, t : t + TILE])

    keep = tri_mask(TILE)

    def head(h, carry):
        kv = h // (HEADS // KV_HEADS)
        rows = pl.ds(pl.multiple_of(h * HEAD, HEAD), HEAD)
        krows = pl.ds(pl.multiple_of(KV0 + kv * HEAD, HEAD), HEAD)
        vrows = pl.ds(pl.multiple_of(V0 + kv * HEAD, HEAD), HEAD)
        for t in range(0, length, TILE):
            cols = slice(t, t + TILE)
            q = qkv_ref[0, rows, cols]
            do = do_ref[0, rows, cols]
            lse = lse_ref[0, pl.ds(h, 1), cols]
            delta = delta_ref[0, pl.ds(h, 1), cols]
            p = jnp.where(keep, jnp.exp(nn(krow[kv, cols, :], q) - lse), 0.0)
            ds = (p * (nn(vrow[kv, cols, :], do) - delta)).astype(BF)
            grads[vrows, cols] += nt(do, p.astype(BF))
            grads[krows, cols] += nt(q, ds)
            dq = nn(qkv_ref[0, krows, cols], ds)
            if t:
                p = jnp.exp(nn(krow[kv, 0:t, :], q) - lse)
                ds = (p * (nn(vrow[kv, 0:t, :], do) - delta)).astype(BF)
                grads[vrows, 0:t] += nt(do, p.astype(BF))
                grads[krows, 0:t] += nt(q, ds)
                dq = dq + nn(qkv_ref[0, krows, 0:t], ds)
            grads[rows, cols] = dq * 0.125
        return carry

    lax.fori_loop(0, HEADS, head, 0)

    gain = gain_ref[...]
    w = w_ref[...]
    for k in range(slices):
        at = pl.multiple_of((me ^ k) * span, span)
        cols = pl.ds(at, span)
        cos = cos_ref[:, cols]
        sin = sin_ref[:, cols]
        parts = []
        for j in range(HEADS + KV_HEADS):
            g1 = grads[j * HEAD : j * HEAD + HALF, cols]
            g2 = grads[j * HEAD + HALF : (j + 1) * HEAD, cols]
            parts.append((g1 * cos + g2 * sin).astype(BF))
            parts.append((g2 * cos - g1 * sin).astype(BF))
        parts.append(grads[V0:, cols].astype(BF))
        dp = jnp.concatenate(parts, axis=0)
        x = xt_ref[0, :, cols].astype(F32)
        inv = inverse_rms(x)
        n = x * inv
        normed = (n * gain).astype(BF)
        acc[...] += nt(normed, dp)
        dh = nn(w, dp)
        dhn = dh * n
        part = dhn[:, 0:128]
        for c in range(128, span, 128):
            part = part + dhn[:, c : c + 128]
        gg_ref[...] += part
        e = dh * gain
        gin = dr_ref[0, :, cols] + inv * (e - n * (jnp.sum(e * n, axis=0, keepdims=True) * (1.0 / D)))
        gin_ref[k, 0] = unflip(gin.astype(BF))

    @pl.when(pl.program_id(0) == pl.num_programs(0) - 1)
    def _():
        gqkv_ref[...] = acc[...].astype(BF)


WHOLE = pl.BlockSpec(memory_space=pltpu.VMEM)


def attention_forward(me, x_stack, wt, gain, cos, sin):
    slices, seqs, span, _ = x_stack.shape
    length = slices * span
    by_seq = lambda rows: pl.BlockSpec((1, rows, length), lambda s, me: (s, 0, 0))
    return pl.pallas_call(
        forward_kernel,
        grid_spec=pltpu.PrefetchScalarGridSpec(
            num_scalar_prefetch=1,
            grid=(seqs,),
            in_specs=[
                pl.BlockSpec((slices, 1, span, D), lambda s, me: (0, s, 0, 0)),
                WHOLE, WHOLE, WHOLE, WHOLE,
            ],
            out_specs=[by_seq(D), by_seq(QKVW), by_seq(D), by_seq(HEADS)],
            scratch_shapes=[pltpu.VMEM((KV_HEADS, length, HEAD), BF)],
        ),
        out_shape=[
            jax.ShapeDtypeStruct((seqs, D, length), BF),
            jax.ShapeDtypeStruct((seqs, QKVW, length), BF),
            jax.ShapeDtypeStruct((seqs, D, length), BF),
            jax.ShapeDtypeStruct((seqs, HEADS, length), F32),
        ],
        compiler_params=pltpu.CompilerParams(vmem_limit_bytes=48 << 20),
        cost_estimate=pl.CostEstimate(
            flops=seqs * (2 * length * D * QKVW + 6 * HEADS * length * length * HEAD),
            bytes_accessed=seqs * length * 7000,
            transcendentals=seqs * HEADS * length * length // 2,
        ),
        name="attention_forward",
    )(me, x_stack, wt, gain, cos, sin)


def middle(me, xt, o, dy_stack, wo, wgu, wd, gain):
    slices, seqs, span, _ = dy_stack.shape
    length = slices * span
    tile = lambda rows: pl.BlockSpec((1, rows, span), lambda s, k, me: (s, 0, k ^ me[0]))
    stacked = pl.BlockSpec((1, 1, span, D), lambda s, k, me: (k, s, 0, 0))
    return pl.pallas_call(
        middle_kernel,
        grid_spec=pltpu.PrefetchScalarGridSpec(
            num_scalar_prefetch=1,
            grid=(seqs, slices),
            in_specs=[tile(D), tile(D), stacked, WHOLE, WHOLE, WHOLE, WHOLE],
            out_specs=[stacked, tile(D), tile(D), tile(HEADS), WHOLE, WHOLE, WHOLE, WHOLE],
            scratch_shapes=[
                pltpu.VMEM((D, D), BF),
                pltpu.VMEM((2 * FF, D), BF),
                pltpu.VMEM((D, FF), BF),
                pltpu.VMEM((D, D), F32),
                pltpu.VMEM((D, 2 * FF), F32),
                pltpu.VMEM((FF, D), F32),
            ],
        ),
        out_shape=[
            jax.ShapeDtypeStruct((slices, seqs, span, D), BF),
            jax.ShapeDtypeStruct((seqs, D, length), F32),
            jax.ShapeDtypeStruct((seqs, D, length), BF),
            jax.ShapeDtypeStruct((seqs, HEADS, length), F32),
            jax.ShapeDtypeStruct((D, D), BF),
            jax.ShapeDtypeStruct((D, 2 * FF), BF),
            jax.ShapeDtypeStruct((FF, D), BF),
            jax.ShapeDtypeStruct((D, 128), F32),
        ],
        compiler_params=pltpu.CompilerParams(vmem_limit_bytes=60 << 20),
        cost_estimate=pl.CostEstimate(
            flops=seqs * length * 6 * (D * D + 3 * D * FF),
            bytes_accessed=seqs * length * 8000 + 12000000,
            transcendentals=seqs * length * FF,
        ),
        name="middle",
    )(me, xt, o, dy_stack, wo, wgu, wd, gain)


def attention_backward(me, xt, qkv, do, lse, delta, dr, w, gain, cos, sin, slices):
    seqs, _, length = xt.shape
    span = length // slices
    by_seq = lambda rows: pl.BlockSpec((1, rows, length), lambda s, me: (s, 0, 0))
    return pl.pallas_call(
        backward_kernel,
        grid_spec=pltpu.PrefetchScalarGridSpec(
            num_scalar_prefetch=1,
            grid=(seqs,),
            in_specs=[
                by_seq(D), by_seq(QKVW), by_seq(D), by_seq(HEADS), by_seq(HEADS), by_seq(D),
                WHOLE, WHOLE, WHOLE, WHOLE,
            ],
            out_specs=[
                pl.BlockSpec((slices, 1, span, D), lambda s, me: (0, s, 0, 0)),
                WHOLE, WHOLE,
            ],
            scratch_shapes=[
                pltpu.VMEM((KV_HEADS, length, HEAD), BF),
                pltpu.VMEM((KV_HEADS, length, HEAD), BF),
                pltpu.VMEM((QKVW, length), F32),
                pltpu.VMEM((D, QKVW), F32),
            ],
        ),
        out_shape=[
            jax.ShapeDtypeStruct((slices, seqs, span, D), BF),
            jax.ShapeDtypeStruct((D, QKVW), BF),
            jax.ShapeDtypeStruct((D, 128), F32),
        ],
        compiler_params=pltpu.CompilerParams(vmem_limit_bytes=56 << 20),
        cost_estimate=pl.CostEstimate(
            flops=seqs * (4 * length * D * QKVW + 10 * HEADS * length * length * HEAD),
            bytes_accessed=seqs * length * 9000,
            transcendentals=seqs * HEADS * length * length // 2,
        ),
        name="attention_backward",
    )(me, xt, qkv, do, lse, delta, dr, w, gain, cos, sin)


def local(tokens, w_qkv, w_out, w_gate_up, w_down, gains, cotangent):
    both = ("dp", "ctx")
    slices = lax.axis_size("ctx")
    world = slices * lax.axis_size("dp")
    span = tokens.shape[1]
    seqs = tokens.shape[0] // slices
    length = slices * span
    me = jnp.zeros((1,), jnp.int32)

    def swap(array):
        return lax.all_to_all(array, "ctx", split_axis=0, concat_axis=0, tiled=True)

    def scatter_sum(terms):
        terms = jnp.pad(terms, ((0, 0), (0, -terms.shape[1] % 128)))
        return lax.psum_scatter(
            terms.reshape(world, -1, 128), both, scatter_dimension=0, tiled=True
        ).reshape(-1)

    first = lax.all_gather(jnp.concatenate([w_qkv, gains]), both, axis=0, tiled=False)
    mat_qkv = first[:, : w_qkv.shape[0]].reshape(D, QKVW)
    gain_all = first[:, w_qkv.shape[0] :].reshape(2, D, 1).astype(F32)
    x_stack = swap(tokens).reshape(slices, seqs, span, D)
    rest = lax.all_gather(jnp.concatenate([w_out, w_gate_up, w_down]), both, axis=0, tiled=False)
    c1 = w_out.shape[0]
    c2 = c1 + w_gate_up.shape[0]
    mat_out = rest[:, :c1].reshape(D, D)
    mat_gu = rest[:, c1:c2].reshape(D, 2 * FF)
    mat_down = rest[:, c2:].reshape(FF, D)
    cos, sin = rotary_tables(length)
    xt, qkv, o, lse = attention_forward(me, x_stack, mat_qkv.T, gain_all[0], cos, sin)
    dy_stack = swap(cotangent).reshape(slices, seqs, span, D)
    out_stack, dr, do, delta, g_out, g_gu, g_down, gg2 = middle(
        me, xt, o, dy_stack, mat_out, mat_gu, mat_down, gain_all[1]
    )
    output = swap(out_stack.reshape(slices * seqs, span, D))
    packed = jnp.concatenate(
        [g_out.reshape(world, -1), g_gu.reshape(world, -1), g_down.reshape(world, -1)], axis=1
    )
    owned = scatter_sum(packed)
    gin_stack, g_qkv, gg1 = attention_backward(
        me, xt, qkv, do, lse, delta, dr, mat_qkv, gain_all[0], cos, sin, slices
    )
    grad_input = swap(gin_stack.reshape(slices * seqs, span, D))
    gg = jnp.concatenate([jnp.sum(gg1, axis=1), jnp.sum(gg2, axis=1)]).astype(BF)
    late = jnp.concatenate([g_qkv.reshape(world, -1), gg.reshape(world, -1)], axis=1)
    owned_late = scatter_sum(late)
    n_qkv = w_qkv.shape[0]
    return (
        output,
        grad_input,
        owned_late[:n_qkv].astype(F32),
        owned[:c1].astype(F32),
        owned[c1:c2].astype(F32),
        owned[c2 : c2 + w_down.shape[0]].astype(F32),
        owned_late[n_qkv : n_qkv + gains.shape[0]].astype(F32),
    )


def solution(mesh):
    flat = P(("dp", "ctx"))
    rows = P("dp", "ctx", None)
    return jax.shard_map(
        local,
        mesh=mesh,
        in_specs=(rows, flat, flat, flat, flat, flat, rows),
        out_specs=(rows, rows, flat, flat, flat, flat, flat),
        check_vma=False,
    )
```

time: 955 us -> 729 us (0.76)
  matrix products: 291 us -> 0 us
  Pallas kernels: 0 us -> 184 us
  other arithmetic: 143 us -> 18.8 us
  waiting for transfers between devices: 265 us -> 371 us
  blocking collectives: 130 us -> 36 us
  local copies, waits for them, and re-layouts: 103 us -> 80.9 us
  starting transfers between devices: 0.24 us -> 12.8 us
    dot_general x18 -> x0, matrix products: 291 us -> none  [the longest x1 57.9 us: local(): jnp.einsum('sqhgd,skhd->shgqk', grad_mixed_low, value_all, preferred_elem...]
    pallas_call x0 -> x3, Pallas kernels: none -> 184 us  [the longest x1 79.6 us: middle(): pl.pallas_call(middle_kernel, grid_spec=pltpu.PrefetchScalarGridSpec(num_...]
    reduce_scatter x1, waiting for transfers between devices: 0.01 us -> 144 us  [scatter_sum(): lax.psum_scatter(terms.reshape(world, -1, 128), both, scatter_dimension=0...]
    unnamed x2 -> x0, blocking collectives: 83.4 us -> none
    convert_element_type x6 -> x7, other arithmetic: 67.4 us -> 6.36 us  [the longest x1 1.61 us: local(): owned[c1:c2].astype(F32)]
    all_gather x1 -> x0, blocking collectives: 46.3 us -> none  [fetch(): lax.all_gather(part_out, ('dp', 'ctx'), axis=0, tiled=True)]
    all_gather x4 -> x1, waiting for transfers between devices: 78 us -> 34.9 us  [local(): lax.all_gather(jnp.concatenate([w_out, w_gate_up, w_down]), both, axis=0,...]
    all_to_all x0 -> x1, blocking collectives: none -> 36 us  [swap(): return lax.all_to_all(array, 'ctx', split_axis=0, concat_axis=0, tiled=True)]
  transfers between devices with their start and end apart: 6 -> 7, of which waited for: 4 -> 5; matrix products, arithmetic and copies ran while one was open for 17% -> 6% of each run, Pallas kernels for 0% -> 6%
where the time goes in v1:
time: 729 us; the launch traced here: 718 us
  waiting for transfers between devices  371 us (51%)
  Pallas kernels  184 us (25%)
  local copies, waits for them, and re-layouts  80.9 us (11%)
  blocking collectives  36 us (5%)
  other arithmetic  18.8 us (3%)
  between operations  14.2 us (2%)
  starting transfers between devices  12.8 us (2%)
    unnamed x6, waiting for transfers between devices  168 us
    reduce_scatter x1, waiting for transfers between devices, scatter_sum(): lax.psum_scatter(terms.reshape(world, -1, 128), both, scatter_dimension=0...  144 us
    pallas_call x1, Pallas kernels, middle(): pl.pallas_call(middle_kernel, grid_spec=pltpu.PrefetchScalarGridSpec(num_...  79.6 us
    pallas_call x1, Pallas kernels, attention_backward(): pl.pallas_call(backward_kernel, grid_spec=pltpu.PrefetchScalarGridSpec(nu...  62.3 us
    pallas_call x1, Pallas kernels, attention_forward(): pl.pallas_call(forward_kernel, grid_spec=pltpu.PrefetchScalarGridSpec(num...  42.1 us
    all_to_all x1, blocking collectives, swap(): return lax.all_to_all(array, 'ctx', split_axis=0, concat_axis=0, tiled=True)  36 us
    all_gather x1, waiting for transfers between devices, local(): lax.all_gather(jnp.concatenate([w_out, w_gate_up, w_down]), both, axis=0,...  34.9 us
    all_to_all x3, waiting for transfers between devices, swap(): return lax.all_to_all(array, 'ctx', split_axis=0, concat_axis=0, tiled=True)  25 us
  transfers between devices with their start and end apart: 7, of which 5 were waited for; matrix products, arithmetic and copies ran while one was open for 6% of the time, Pallas kernels for 6%

profile of v1, /device:TPU:0, one launch (start us, length us, event | category | flops | bytes accessed | tf_op | source)
XLA Modules:
  0.0 717.8 jit_solution(514582788770485234)
XLA Ops:
  7.3 0.8 pad_maximum_fusion.2
  8.7 1.0 copy-done.6
  9.9 0.9 reshape.129
  10.8 36.0 %all_to_all.20 = bf16[8,256,576]{1,2,0:T(8,128)(2,1)} all-to-all(bf16[8,256,576]{1,2,0:T(8,128)(2,1)} %param.7), channel_id=1, replica_groups=mesh['dp'=8,'ctx'=4] {'ctx'}, dimensions={0} | all-to-all | bytes 4718592 | tf_op jit(solution)/shard_map/all_to_all | solution.py:402
  46.8 4.5 all-to-all-start.1
  52.0 95.0 %all-reduce.6.cloned.1.call-done = bf16[554112]{0:T(1024)(128)(2,1)} async-done(((bf16[554112]{0:T(1024)(128)(2,1)}), bf16[554112]{0:T(1024)(128)(2,1)}) %all-reduce.6.cloned.1.call-update) | async-done | bytes 1108240
  147.0 2.7 reshape.125
  149.7 1.1 slice.55
  150.9 2.2 reshape.107.w_ref
  153.2 1.1 copy.36.wt_ref
  154.3 0.9 squeeze.10.gain_ref
  155.2 4.3 copy.35
  159.6 4.4 copy.38
  164.0 42.1 %attention_forward.1 = (bf16[2,576,1024]{2,1,0:T(8,128)(2,1)S(1)}, bf16[2,960,1024]{2,1,0:T(8,128)(2,1)}, bf16[2,576,1024]{2,1,0:T(8,128)(2,1)}, f32[2,9,1024]{2,1,0:T(8,128)S(1)}) custom-call(s32[1]{0:T(128)} %constant.5.clone.1.me_ref, bf16[4,2,256,576]{3,2,1,0:T(8,128)(2,1)} %bitcast.41, bf16[960,576]{1,0:T(8,128)(2,1)S(1)} %copy.36.wt_ref, ...), custom_call_target="tpu_custom_call" | custom-call | flops 9512681472 | bytes 14336000 | tf_op jit(solution)/shard_map/attention_forward/pallas_call | solution.py:284
  206.1 1.4 copy-done.3
  208.1 34.9 %all-gather.5.cloned.1.call-done = bf16[32,1,93312]{2,1,0:T(2,128)(2,1)} async-done(((bf16[1,1,93312]{2,1,0:T(2,128)(2,1)}), bf16[32,1,93312]{2,1,0:T(2,128)(2,1)}) %all-gather.5.cloned.1.call-update) | async-done | bytes 5971984 | tf_op jit(solution)/shard_map/all_gather | solution.py:414
  243.0 5.0 copy.46
  248.1 2.0 slice.59
  250.2 0.9 slice.58
  251.1 7.7 %reshape.110.wgu_ref = bf16[576,3072]{1,0:T(8,128)(2,1)} reshape(bf16[32,55296]{1,0:T(8,128)(2,1)} %slice.59) | data formatting | bytes 7077888 | tf_op jit(solution)/shard_map/reshape | solution.py:418
  258.8 2.6 reshape.111.wd_ref
  261.3 1.7 reshape.109.wo_ref
  263.1 79.6 %middle.1 = (bf16[4,2,256,576]{3,2,1,0:T(8,128)(2,1)}, f32[2,576,1024]{2,1,0:T(8,128)}, bf16[2,576,1024]{2,1,0:T(8,128)(2,1)}, f32[2,9,1024]{2,1,0:T(8,128)}, bf...) custom-call(s32[1]{0:T(128)} %constant.5.clone.1.me_ref, ...), custom_call_target="tpu_custom_call" | custom-call | flops 36691771392 | bytes 28384000 | tf_op jit(solution)/shard_map/middle/pallas_call | solution.py:317
  342.7 6.6 reshape.117
  349.3 4.1 reshape.118
  353.4 2.6 reshape.116
  356.0 62.3 %attention_backward.1 = (bf16[4,2,256,576]{3,2,1,0:T(8,128)(2,1)}, bf16[576,960]{1,0:T(8,128)(2,1)}, f32[576,128]{1,0:T(8,128)}) custom-call(s32[1]{0:T(128)} %constant.5.clone.1.me_ref, bf16[2,576,1024]{2,1,0:T(8,128)(2,1)} %copy-done.3, bf16[2,960,1024]{2,1,0:T(8,128)(2,1)} %get-tuple-element.25.qkv_ref, bf16[2,576,1024]{2,1,0:T(8,128)(2,1)} %get-tuple-element.26.do_ref, ...), custom_call_target="tpu_custom_call" | custom-call | flops 16609443840 | bytes 18432000 | tf_op jit(solution)/shard_map/attention_backward/pallas_call | solution.py:357
  418.3 3.5 reshape.114
  421.8 1.1 reduce_sum.18
  423.0 1.1 reduce_sum.19
  424.2 1.3 fusion.4
  425.6 1.2 copy.44
  426.8 7.4 %pad_maximum_fusion = bf16[32,93312]{1,0:T(8,128)(2,1)} fusion(bf16[32,27648]{1,0:T(8,128)(2,1)} %reshape.118, bf16[32,55296]{1,0:T(8,128)(2,1)S(1)} %reshape.117, bf16[32,10368]{1,0:T(8,128)(2,1)} %reshape.116), kind=kLoop, calls=%fused_computation | loop fusion | flops 17915904 | bytes 11943936 | tf_op jit(solution)/shard_map/concatenate | solution.py:427
  434.2 7.1 reshape.119
  441.3 1.7 copy-done.8
  443.1 2.5 copy.42
  445.6 3.6 all-to-all-start.3
  449.3 4.3 copy.40
  453.6 25.0 %all-to-all-done.3 = bf16[8,256,576]{1,2,0:T(8,128)(2,1)S(1)} async-done(((bf16[8,256,576]{1,2,0:T(8,128)(2,1)}), bf16[8,256,576]{1,2,0:T(8,128)(2,1)S(1)}, u32[]{:S(2)}, u32[]{:S(2)}) %all-to-all-start.3) | async-done | bytes 2359328 | tf_op jit(solution)/shard_map/all_to_all | solution.py:402
  478.6 4.5 all-to-all-start.2
  483.2 72.5 %all-reduce.8.cloned.1.call-done = bf16[32,136,128]{2,1,0:T(8,128)(2,1)} async-done(((bf16[32,136,128]{2,1,0:T(8,128)(2,1)}), bf16[32,136,128]{2,1,0:T(8,128)(2,1)}) %all-reduce.8.cloned.1.call-update) | async-done | bytes 1114128
  557.0 1.4 fusion.8
  558.4 143.6 %reduce-scatter.2.cloned.1.call-done = bf16[1,729,128]{2,1,0:T(8,128)(2,1)} async-done(((bf16[32,729,128]{2,1,0:T(8,128)(2,1)}), bf16[1,729,128]{2,1,0:T(8,128)(2,1)}) %reduce-scatter.2.cloned.1.call-update) | async-done | bytes 186640 | tf_op jit(solution)/shard_map/reduce_scatter | solution.py:406
  701.9 1.6 fusion.6
  703.6 1.5 fusion.7
  705.0 1.4 fusion.9
  706.4 3.2 copy.52
  709.6 1.4 copy.53
  (45 shorter events, 3.9 us)
Async XLA Ops:
  7.2 2.6 copy-start.9
  7.2 2.6 copy-start.10
  7.2 2.6 copy-start.11
  7.2 139.8 %all-reduce.6.cloned.1.call-start = ((), (), s32[]{:S(2)}) async-start(), calls=%async_computation.6 | async-start | bytes 2220032
  8.7 1.0 copy-start.6
  9.7 233.3 %all-gather.5.cloned.1.call-start = ((), (), s32[]{:S(2)}) async-start(), calls=%async_computation.7 | async-start | bytes 12317184 | tf_op jit(solution)/shard_map/all_gather | solution.py:414
  46.8 112.7 %all-to-all-start.1 = ((bf16[8,256,576]{1,2,0:T(8,128)(2,1)}), bf16[8,256,576]{1,2,0:T(8,128)(2,1)}, u32[]{:S(2)}, u32[]{:S(2)}) async-start(bf16[8,256,576]{1,2,0:T(8,128)(2,1)} %param.13), calls=%async_computation.1 | async-start | bytes 4718592 | tf_op jit(solution)/shard_map/all_to_all | solution.py:402
  51.3 504.4 %all-reduce.8.cloned.1.call-start = ((), (), s32[]{:S(2)}) async-start(), calls=%async_computation.8 | async-start | bytes 2228224
  51.9 112.0 %copy-start.1 = (f32[32,1024]{1,0:T(8,128)}, f32[32,1024]{1,0:T(8,128)S(1)}, u32[]{:S(2)}) copy-start(f32[32,1024]{1,0:T(8,128)S(1)} %get-tuple-element.39.sin_ref) | copy-start | bytes 393220
  52.0 112.0 %copy-start.2 = (f32[32,1024]{1,0:T(8,128)}, f32[32,1024]{1,0:T(8,128)S(1)}, u32[]{:S(2)}) copy-start(f32[32,1024]{1,0:T(8,128)S(1)} %get-tuple-element.40.cos_ref) | copy-start | bytes 393220
  150.9 13.0 %copy-start = (f32[576,1]{1,0:T(8,128)}, f32[576,1]{1,0:T(8,128)S(1)}, u32[]{:S(2)}) copy-start(f32[576,1]{1,0:T(8,128)S(1)} %squeeze.9.gain_ref) | copy-start | bytes 6916
  153.2 6.4 copy-start.5
  206.1 1.4 copy-start.3
  207.5 0.7 copy-start.4
  258.8 2.6 copy-start.7
  426.8 275.2 %reduce-scatter.2.cloned.1.call-start = ((), (), s32[]{:S(2)}) async-start(), calls=%async_computation.5 | async-start | bytes 6217728 | tf_op jit(solution)/shard_map/reduce_scatter | solution.py:406
  441.3 1.8 copy-start.8
  445.6 33.0 %all-to-all-start.3 = ((bf16[8,256,576]{1,2,0:T(8,128)(2,1)}), bf16[8,256,576]{1,2,0:T(8,128)(2,1)S(1)}, u32[]{:S(2)}, u32[]{:S(2)}) async-start(bf16[8,256,576]{1,2,0:T(8,128)(2,1)} %copy.42), calls=%async_computation.3 | async-start | bytes 4718592 | tf_op jit(solution)/shard_map/all_to_all | solution.py:402
  478.6 79.8 %all-to-all-start.2 = ((bf16[8,256,576]{1,2,0:T(8,128)(2,1)}), bf16[8,256,576]{1,2,0:T(8,128)(2,1)}, u32[]{:S(2)}, u32[]{:S(2)}) async-start(bf16[8,256,576]{1,2,0:T(8,128)(2,1)} %copy.40), calls=%async_computation.2 | async-start | bytes 4718592 | tf_op jit(solution)/shard_map/all_to_all | solution.py:402
Sparse Core Ops, SparseCore 0:
  14.0 132.8 all-reduce.5
  150.3 92.7 all-gather.4
  426.9 128.7 all-reduce.7
  557.8 144.0 reduce-scatter.1

commit v2 on v1

--- a/solution.py
+++ b/solution.py
@@ -1,3 +1,4 @@
+import functools
 import math
 
 import jax
@@ -69,21 +70,105 @@
     return key <= query
 
 
-def forward_kernel(me_ref, x_ref, wt_ref, gain_ref, cos_ref, sin_ref, xt_ref, qkv_ref, o_ref, lse_ref, krow):
-    slices, _, span, _ = x_ref.shape
+def lane_low(size):
+    return lax.broadcasted_iota(jnp.int32, (size, 128), 1) < 64
+
+
+def to_flat(rows_ref, flat_ref, rows, width):
+    if width % 128 == 0:
+        n = width // 128
+
+        @pl.loop(0, n)
+        def _(c):
+            flat_ref[pl.ds(c, rows, stride=n), :] = rows_ref[:, pl.ds(pl.multiple_of(c * 128, 128), 128)]
+
+        return
+    n = 2 * width // 128
+    half = rows // 2
+    low = lane_low(half)
+    even = lambda c: rows_ref[c, pl.ds(0, half, stride=2), :]
+    odd = lambda c: pltpu.roll(rows_ref[c, pl.ds(1, half, stride=2), :], 64, 1)
+    for c in range(n // 2):
+        flat_ref[pl.ds(c, half, stride=n), :] = even(c)
+    before = odd(0)
+    flat_ref[pl.ds(n // 2, half, stride=n), :] = jnp.where(low, even(n // 2), before)
+    for c in range(n // 2):
+        after = odd(c + 1)
+        flat_ref[pl.ds(n // 2 + 1 + c, half, stride=n), :] = jnp.where(low, before, after)
+        before = after
+
+
+def from_flat(flat_ref, rows_ref, rows, width):
+    if width % 128 == 0:
+        n = width // 128
+
+        @pl.loop(0, n)
+        def _(c):
+            rows_ref[:, pl.ds(pl.multiple_of(c * 128, 128), 128)] = flat_ref[
+                pl.ds(c, rows, stride=n), :
+            ].astype(rows_ref.dtype)
+
+        return
+    n = 2 * width // 128
+    half = rows // 2
+    low = lane_low(half)
+    take = lambda c: flat_ref[pl.ds(c, half, stride=n), :]
+    for c in range(n // 2 + 1):
+        rows_ref[c, pl.ds(0, half, stride=2), :] = take(c)
+    before = pltpu.roll(take(n // 2), 64, 1)
+    for c in range(n // 2):
+        after = pltpu.roll(take(n // 2 + 1 + c), 64, 1)
+        rows_ref[c, pl.ds(1, half, stride=2), :] = jnp.where(low, before, after)
+        before = after
+    rows_ref[n // 2, pl.ds(1, half, stride=2), :] = before
+
+
+def convert(src_ref, dst_ref, rows, step):
+    @pl.loop(0, rows, step=step)
+    def _(i):
+        at = pl.ds(pl.multiple_of(i, step), step)
+        dst_ref[at, :] = src_ref[at, 0 : dst_ref.shape[1]].astype(dst_ref.dtype)
+
+
+def clear(ref, step):
+    @pl.loop(0, ref.shape[-2], step=step)
+    def _(i):
+        at = pl.ds(pl.multiple_of(i, step), step)
+        if len(ref.shape) == 3:
+            ref[:, at, :] = jnp.zeros((ref.shape[0], step, ref.shape[2]), ref.dtype)
+        else:
+            ref[at, :] = jnp.zeros((step, ref.shape[1]), ref.dtype)
+
+
+def add_chunks(ref, value):
+    for c, w in col_chunks(value.shape[1]):
+        ref[c // 128, :, 0:w] += value[:, c : c + w]
+
+
+def join_chunks(src_ref, dst_ref):
+    for c, w in col_chunks(dst_ref.shape[1]):
+        dst_ref[:, c : c + w] = src_ref[c // 128, :, 0:w].astype(dst_ref.dtype)
+
+
+def forward_kernel(slices, me_ref, *refs):
+    x_refs = refs[:slices]
+    wt_ref, gain_ref, cos_ref, sin_ref, xt_ref, qkv_ref, o_ref, lse_ref, krow = refs[slices:]
+    _, span, _ = x_refs[0].shape
     length = slices * span
     me = me_ref[0]
     for k in range(slices):
         at = pl.multiple_of((me ^ k) * span, span)
-        xt_ref[0, :, pl.ds(at, span)] = flip(x_ref[k, 0])
+        xt_ref[0, :, pl.ds(at, span)] = flip(x_refs[k][0])
     gain = gain_ref[...]
-    wt = wt_ref[...]
-    for t in range(0, length, TILE):
-        x = xt_ref[0, :, t : t + TILE].astype(F32)
+
+    @pl.loop(0, length, step=TILE)
+    def _(start):
+        tok = pl.ds(pl.multiple_of(start, TILE), TILE)
+        x = xt_ref[0, :, tok].astype(F32)
         normed = (x * inverse_rms(x) * gain).astype(BF)
-        proj = nn(wt, normed)
-        cos = cos_ref[:, t : t + TILE]
-        sin = sin_ref[:, t : t + TILE]
+        proj = nn(wt_ref[...], normed)
+        cos = cos_ref[:, tok]
+        sin = sin_ref[:, tok]
         for j in range(HEADS + KV_HEADS):
             u1 = proj[j * HEAD : j * HEAD + HALF]
             u2 = proj[j * HEAD + HALF : (j + 1) * HEAD]
@@ -92,11 +177,11 @@
             if j < HEADS:
                 r1 = r1 * jnp.asarray(0.125, BF)
                 r2 = r2 * jnp.asarray(0.125, BF)
-            qkv_ref[0, j * HEAD : j * HEAD + HALF, t : t + TILE] = r1
-            qkv_ref[0, j * HEAD + HALF : (j + 1) * HEAD, t : t + TILE] = r2
-        qkv_ref[0, V0:, t : t + TILE] = proj[V0:].astype(BF)
+            qkv_ref[0, j * HEAD : j * HEAD + HALF, tok] = r1
+            qkv_ref[0, j * HEAD + HALF : (j + 1) * HEAD, tok] = r2
+        qkv_ref[0, V0:, tok] = proj[V0:].astype(BF)
         for j in range(KV_HEADS):
-            krow[j, t : t + TILE, :] = unflip(qkv_ref[0, KV0 + j * HEAD : KV0 + (j + 1) * HEAD, t : t + TILE])
+            krow[j, tok, :] = unflip(qkv_ref[0, KV0 + j * HEAD : KV0 + (j + 1) * HEAD, tok])
 
     keep = tri_mask(TILE)
 
@@ -127,23 +212,35 @@
 
 
 def middle_kernel(
-    me_ref, xt_ref, o_ref, dy_ref, wo_ref, wgu_ref, wd_ref, gain_ref,
+    me_ref, xt_ref, o_ref, dy_ref, fo_ref, fgu_ref, fd_ref, gain_ref,
     out_ref, dr_ref, do_ref, delta_ref, gout_ref, ggu_ref, gdown_ref, gg_ref,
-    wot, wgut, wdt, aout, agu, adown,
+    wo_ref, wgu_ref, wd_ref, wot, wgut, wdt, aout, agu, adown,
 ):
     step = pl.program_id(0) * pl.num_programs(1) + pl.program_id(1)
     last = pl.num_programs(0) * pl.num_programs(1) - 1
 
     @pl.when(step == 0)
     def _():
-        for c in range(0, 2 * FF, TILE):
-            wgut[c : c + TILE, :] = nt(eye(TILE), wgu_ref[:, c : c + TILE]).astype(BF)
+        convert(fgu_ref, ggu_ref, fgu_ref.shape[0], 256)
+        from_flat(ggu_ref, wgu_ref, D, 2 * FF)
+        convert(fd_ref, gdown_ref, fd_ref.shape[0], 256)
+        from_flat(gdown_ref, adown, FF, D)
+        join_chunks(adown, wd_ref)
+        convert(fo_ref, gout_ref, fo_ref.shape[0], 96)
+        from_flat(gout_ref, aout, D, D)
+        join_chunks(aout, wo_ref)
+
+        @pl.loop(0, 2 * FF, step=TILE)
+        def _(c):
+            at = pl.ds(pl.multiple_of(c, TILE), TILE)
+            wgut[at, :] = nt(eye(TILE), wgu_ref[:, at]).astype(BF)
+
         for c, w in col_chunks(D):
             wdt[c : c + w, :] = nt(eye(w), wd_ref[:, c : c + w]).astype(BF)
             wot[c : c + w, :] = nt(eye(w), wo_ref[:, c : c + w]).astype(BF)
-        aout[...] = jnp.zeros_like(aout)
-        agu[...] = jnp.zeros_like(agu)
-        adown[...] = jnp.zeros_like(adown)
+        clear(aout, 64)
+        clear(agu, 16)
+        clear(adown, 64)
         gg_ref[...] = jnp.zeros_like(gg_ref)
 
     gain = gain_ref[...]
@@ -160,7 +257,7 @@
     out_ref[0, 0] = unflip((r + nn(wdt[...], m)).astype(BF))
     dy = dy_ref[0, 0]
     dyt = flip(dy)
-    adown[...] += nn(m, dy)
+    add_chunks(adown, nn(m, dy))
     dm = nn(wd_ref[...], dyt)
     da = (dm * u * sg * (1.0 + a * (1.0 - sg))).astype(BF)
     du = (dm * act).astype(BF)
@@ -176,7 +273,7 @@
     dr = dyt.astype(F32) + inv * (e - n * (jnp.sum(e * n, axis=0, keepdims=True) * (1.0 / D)))
     dr_ref[0] = dr
     db = dr.astype(BF)
-    aout[...] += nt(o, db)
+    add_chunks(aout, nt(o, db))
     do = nn(wo_ref[...], db).astype(BF)
     do_ref[0] = do
     prod = do.astype(F32) * o.astype(F32)
@@ -185,9 +282,9 @@
 
     @pl.when(step == last)
     def _():
-        gout_ref[...] = aout[...].astype(BF)
-        ggu_ref[...] = agu[...].astype(BF)
-        gdown_ref[...] = adown[...].astype(BF)
+        to_flat(aout, gout_ref, D, D)
+        to_flat(agu, ggu_ref, D, 2 * FF)
+        to_flat(adown, gdown_ref, FF, D)
 
 
 def backward_kernel(
@@ -199,16 +296,16 @@
     length = slices * span
     me = me_ref[0]
 
-    @pl.when(pl.program_id(0) == 0)
-    def _():
-        acc[...] = jnp.zeros_like(acc)
-        gg_ref[...] = jnp.zeros_like(gg_ref)
-
-    grads[...] = jnp.zeros_like(grads)
-    for t in range(0, length, TILE):
+    clear(acc, 64)
+    gg_ref[...] = jnp.zeros_like(gg_ref)
+    clear(grads, 64)
+
+    @pl.loop(0, length, step=TILE)
+    def _(start):
+        tok = pl.ds(pl.multiple_of(start, TILE), TILE)
         for j in range(KV_HEADS):
-            krow[j, t : t + TILE, :] = unflip(qkv_ref[0, KV0 + j * HEAD : KV0 + (j + 1) * HEAD, t : t + TILE])
-            vrow[j, t : t + TILE, :] = unflip(qkv_ref[0, V0 + j * HEAD : V0 + (j + 1) * HEAD, t : t + TILE])
+            krow[j, tok, :] = unflip(qkv_ref[0, KV0 + j * HEAD : KV0 + (j + 1) * HEAD, tok])
+            vrow[j, tok, :] = unflip(qkv_ref[0, V0 + j * HEAD : V0 + (j + 1) * HEAD, tok])
 
     keep = tri_mask(TILE)
 
@@ -240,8 +337,9 @@
     lax.fori_loop(0, HEADS, head, 0)
 
     gain = gain_ref[...]
-    w = w_ref[...]
-    for k in range(slices):
+
+    @pl.loop(0, slices)
+    def _(k):
         at = pl.multiple_of((me ^ k) * span, span)
         cols = pl.ds(at, span)
         cos = cos_ref[:, cols]
@@ -258,8 +356,8 @@
         inv = inverse_rms(x)
         n = x * inv
         normed = (n * gain).astype(BF)
-        acc[...] += nt(normed, dp)
-        dh = nn(w, dp)
+        add_chunks(acc, nt(normed, dp))
+        dh = nn(w_ref[...], dp)
         dhn = dh * n
         part = dhn[:, 0:128]
         for c in range(128, span, 128):
@@ -269,25 +367,24 @@
         gin = dr_ref[0, :, cols] + inv * (e - n * (jnp.sum(e * n, axis=0, keepdims=True) * (1.0 / D)))
         gin_ref[k, 0] = unflip(gin.astype(BF))
 
-    @pl.when(pl.program_id(0) == pl.num_programs(0) - 1)
-    def _():
-        gqkv_ref[...] = acc[...].astype(BF)
+    to_flat(acc, gqkv_ref, D, QKVW)
 
 
 WHOLE = pl.BlockSpec(memory_space=pltpu.VMEM)
 
 
-def attention_forward(me, x_stack, wt, gain, cos, sin):
-    slices, seqs, span, _ = x_stack.shape
+def attention_forward(me, x_parts, wt, gain, cos, sin):
+    slices = len(x_parts)
+    seqs, span, _ = x_parts[0].shape
     length = slices * span
     by_seq = lambda rows: pl.BlockSpec((1, rows, length), lambda s, me: (s, 0, 0))
     return pl.pallas_call(
-        forward_kernel,
+        functools.partial(forward_kernel, slices),
         grid_spec=pltpu.PrefetchScalarGridSpec(
             num_scalar_prefetch=1,
             grid=(seqs,),
             in_specs=[
-                pl.BlockSpec((slices, 1, span, D), lambda s, me: (0, s, 0, 0)),
+                *[pl.BlockSpec((1, span, D), lambda s, me: (s, 0, 0))] * slices,
                 WHOLE, WHOLE, WHOLE, WHOLE,
             ],
             out_specs=[by_seq(D), by_seq(QKVW), by_seq(D), by_seq(HEADS)],
@@ -306,7 +403,7 @@
             transcendentals=seqs * HEADS * length * length // 2,
         ),
         name="attention_forward",
-    )(me, x_stack, wt, gain, cos, sin)
+    )(me, *x_parts, wt, gain, cos, sin)
 
 
 def middle(me, xt, o, dy_stack, wo, wgu, wd, gain):
@@ -323,11 +420,14 @@
             out_specs=[stacked, tile(D), tile(D), tile(HEADS), WHOLE, WHOLE, WHOLE, WHOLE],
             scratch_shapes=[
                 pltpu.VMEM((D, D), BF),
+                pltpu.VMEM((D, 2 * FF), BF),
+                pltpu.VMEM((FF, D), BF),
+                pltpu.VMEM((D, D), BF),
                 pltpu.VMEM((2 * FF, D), BF),
                 pltpu.VMEM((D, FF), BF),
-                pltpu.VMEM((D, D), F32),
+                pltpu.VMEM((5, D, 128), F32),
                 pltpu.VMEM((D, 2 * FF), F32),
-                pltpu.VMEM((FF, D), F32),
+                pltpu.VMEM((5, FF, 128), F32),
             ],
         ),
         out_shape=[
@@ -335,9 +435,9 @@
             jax.ShapeDtypeStruct((seqs, D, length), F32),
             jax.ShapeDtypeStruct((seqs, D, length), BF),
             jax.ShapeDtypeStruct((seqs, HEADS, length), F32),
-            jax.ShapeDtypeStruct((D, D), BF),
-            jax.ShapeDtypeStruct((D, 2 * FF), BF),
-            jax.ShapeDtypeStruct((FF, D), BF),
+            jax.ShapeDtypeStruct((D * D // 128, 128), F32),
+            jax.ShapeDtypeStruct((D * 2 * FF // 128, 128), F32),
+            jax.ShapeDtypeStruct((FF * D // 128, 128), F32),
             jax.ShapeDtypeStruct((D, 128), F32),
         ],
         compiler_params=pltpu.CompilerParams(vmem_limit_bytes=60 << 20),
@@ -350,100 +450,185 @@
     )(me, xt, o, dy_stack, wo, wgu, wd, gain)
 
 
-def attention_backward(me, xt, qkv, do, lse, delta, dr, w, gain, cos, sin, slices):
-    seqs, _, length = xt.shape
+def attention_backward(seq, me, xt, qkv, do, lse, delta, dr, w, gain, cos, sin, slices):
+    _, _, length = xt.shape
     span = length // slices
-    by_seq = lambda rows: pl.BlockSpec((1, rows, length), lambda s, me: (s, 0, 0))
+    by_seq = lambda rows: pl.BlockSpec((1, rows, length), lambda s, me: (seq, 0, 0))
     return pl.pallas_call(
         backward_kernel,
         grid_spec=pltpu.PrefetchScalarGridSpec(
             num_scalar_prefetch=1,
-            grid=(seqs,),
+            grid=(1,),
             in_specs=[
                 by_seq(D), by_seq(QKVW), by_seq(D), by_seq(HEADS), by_seq(HEADS), by_seq(D),
                 WHOLE, WHOLE, WHOLE, WHOLE,
             ],
             out_specs=[
-                pl.BlockSpec((slices, 1, span, D), lambda s, me: (0, s, 0, 0)),
+                pl.BlockSpec((slices, 1, span, D), lambda s, me: (0, 0, 0, 0)),
                 WHOLE, WHOLE,
             ],
             scratch_shapes=[
                 pltpu.VMEM((KV_HEADS, length, HEAD), BF),
                 pltpu.VMEM((KV_HEADS, length, HEAD), BF),
                 pltpu.VMEM((QKVW, length), F32),
-                pltpu.VMEM((D, QKVW), F32),
+                pltpu.VMEM((8, D, 128), F32),
             ],
         ),
         out_shape=[
-            jax.ShapeDtypeStruct((slices, seqs, span, D), BF),
-            jax.ShapeDtypeStruct((D, QKVW), BF),
+            jax.ShapeDtypeStruct((slices, 1, span, D), BF),
+            jax.ShapeDtypeStruct((D * QKVW // 128, 128), F32),
             jax.ShapeDtypeStruct((D, 128), F32),
         ],
         compiler_params=pltpu.CompilerParams(vmem_limit_bytes=56 << 20),
         cost_estimate=pl.CostEstimate(
-            flops=seqs * (4 * length * D * QKVW + 10 * HEADS * length * length * HEAD),
-            bytes_accessed=seqs * length * 9000,
-            transcendentals=seqs * HEADS * length * length // 2,
+            flops=4 * length * D * QKVW + 10 * HEADS * length * length * HEAD,
+            bytes_accessed=length * 9000,
+            transcendentals=HEADS * length * length // 2,
         ),
         name="attention_backward",
     )(me, xt, qkv, do, lse, delta, dr, w, gain, cos, sin)
 
 
+def place_kernel(me_ref, *refs):
+    parts, out_ref, sems = refs[:-2], refs[-2], refs[-1]
+    copies = [
+        pltpu.make_async_copy(part, out_ref.at[me_ref[0] ^ k], sems.at[k]) for k, part in enumerate(parts)
+    ]
+    for copy in copies:
+        copy.start()
+    for copy in copies:
+        copy.wait()
+
+
+def place(me, parts):
+    any_space = pl.BlockSpec(memory_space=pl.ANY)
+    return pl.pallas_call(
+        place_kernel,
+        grid_spec=pltpu.PrefetchScalarGridSpec(
+            num_scalar_prefetch=1,
+            grid=(1,),
+            in_specs=[any_space] * len(parts),
+            out_specs=any_space,
+            scratch_shapes=[pltpu.SemaphoreType.DMA((len(parts),))],
+        ),
+        out_shape=jax.ShapeDtypeStruct((len(parts),) + parts[0].shape, parts[0].dtype),
+        cost_estimate=pl.CostEstimate(flops=0, bytes_accessed=4 * len(parts) * parts[0].size, transcendentals=0),
+        name="place",
+    )(me, *parts)
+
+
+def partner(array, name, bits):
+    return lax.ppermute(array, name, [(i, i ^ bits) for i in range(lax.axis_size(name))])
+
+
+def digit_of(name, stride, count):
+    return (lax.axis_index(name) // stride) % count
+
+
+def gather_digit(array, name, stride, count):
+    parts = [array] + [partner(array, name, k * stride) for k in range(1, count)]
+    digit = digit_of(name, stride, count)
+    bit = 1
+    while bit < count:
+        swap = (digit & bit) != 0
+        parts = [jnp.where(swap, parts[k ^ bit], parts[k]) for k in range(count)]
+        bit *= 2
+    return jnp.stack(parts)
+
+
+def sum_digit(terms, axis, name, stride, count, dtype):
+    digit = digit_of(name, stride, count)
+    total = lax.dynamic_index_in_dim(terms, digit, axis, keepdims=False).astype(F32)
+    for k in range(1, count):
+        piece = lax.dynamic_index_in_dim(terms, digit ^ k, axis, keepdims=False).astype(BF)
+        total = total + partner(piece, name, k * stride).astype(F32)
+    return total.astype(dtype)
+
+
 def local(tokens, w_qkv, w_out, w_gate_up, w_down, gains, cotangent):
     both = ("dp", "ctx")
     slices = lax.axis_size("ctx")
-    world = slices * lax.axis_size("dp")
+    across = lax.axis_size("dp")
+    world = slices * across
     span = tokens.shape[1]
     seqs = tokens.shape[0] // slices
     length = slices * span
-    me = jnp.zeros((1,), jnp.int32)
-
-    def swap(array):
-        return lax.all_to_all(array, "ctx", split_axis=0, concat_axis=0, tiled=True)
-
-    def scatter_sum(terms):
-        terms = jnp.pad(terms, ((0, 0), (0, -terms.shape[1] % 128)))
-        return lax.psum_scatter(
-            terms.reshape(world, -1, 128), both, scatter_dimension=0, tiled=True
-        ).reshape(-1)
-
-    first = lax.all_gather(jnp.concatenate([w_qkv, gains]), both, axis=0, tiled=False)
-    mat_qkv = first[:, : w_qkv.shape[0]].reshape(D, QKVW)
-    gain_all = first[:, w_qkv.shape[0] :].reshape(2, D, 1).astype(F32)
-    x_stack = swap(tokens).reshape(slices, seqs, span, D)
-    rest = lax.all_gather(jnp.concatenate([w_out, w_gate_up, w_down]), both, axis=0, tiled=False)
-    c1 = w_out.shape[0]
-    c2 = c1 + w_gate_up.shape[0]
-    mat_out = rest[:, :c1].reshape(D, D)
-    mat_gu = rest[:, c1:c2].reshape(D, 2 * FF)
-    mat_down = rest[:, c2:].reshape(FF, D)
+    ctx = lax.axis_index("ctx")
+    me = ctx.astype(jnp.int32).reshape(1)
+    nz = min(4, across)
+    nx = across // nz
+    core = ("ctx", 1, 2)
+    y = ("ctx", 2, slices // 2)
+    x = ("dp", 1, nx)
+    z = ("dp", nx, nz)
+
+    def exchange(array):
+        grouped = array.reshape(slices, seqs, span, D)
+        parts = [lax.dynamic_index_in_dim(grouped, ctx ^ k, 0, keepdims=False) for k in range(slices)]
+        return parts[:1] + [partner(parts[k], "ctx", k) for k in range(1, slices)]
+
+    def give_back(parts):
+        return parts[:1] + [partner(parts[k], "ctx", k) for k in range(1, slices)]
+
+    def reduce_terms(flat, order):
+        terms = flat.reshape(nz, nx, slices // 2, 2, -1, 128)
+        terms = sum_digit(terms, 3, *core, BF)
+        if order == "xy":
+            terms = sum_digit(terms, 1, *x, BF)
+            terms = sum_digit(terms, 1, *y, BF)
+        else:
+            terms = sum_digit(terms, 2, *y, BF)
+            terms = sum_digit(terms, 1, *x, BF)
+        return sum_digit(terms, 0, *z, F32).reshape(-1)
+
+    def shares(flat):
+        rows = flat.reshape(world, -1)
+        return jnp.pad(rows, ((0, 0), (0, -rows.shape[1] % 128)))
+
+    n_qkv = w_qkv.shape[0]
+    n_gain = gains.shape[0]
+    early = jnp.concatenate([w_qkv, gains])
+    early = jnp.pad(early, (0, -early.shape[0] % 1024)).reshape(-1, 128)
+    for digit in (y, z, x, core):
+        early = gather_digit(early, *digit)
+    early = early.reshape(2, nx, nz, slices // 2, -1).transpose(2, 1, 3, 0, 4).reshape(world, -1)
+    mat_qkv = early[:, :n_qkv].reshape(D, QKVW)
+    gain_all = early[:, n_qkv : n_qkv + n_gain].reshape(2, D, 1).astype(F32)
+    x_parts = exchange(tokens)
+    rest = lax.all_gather(jnp.concatenate([w_gate_up, w_down, w_out]), both, axis=0, tiled=False)
+    c1 = w_gate_up.shape[0]
+    c2 = c1 + w_down.shape[0]
+    flat_gu = rest[:, :c1].reshape(-1, 128)
+    flat_down = rest[:, c1:c2].reshape(-1, 128)
+    flat_out = rest[:, c2:].reshape(-1, 128)
     cos, sin = rotary_tables(length)
-    xt, qkv, o, lse = attention_forward(me, x_stack, mat_qkv.T, gain_all[0], cos, sin)
-    dy_stack = swap(cotangent).reshape(slices, seqs, span, D)
+    xt, qkv, o, lse = attention_forward(me, x_parts, mat_qkv.T, gain_all[0], cos, sin)
+    dy_stack = jnp.stack(exchange(cotangent))
     out_stack, dr, do, delta, g_out, g_gu, g_down, gg2 = middle(
-        me, xt, o, dy_stack, mat_out, mat_gu, mat_down, gain_all[1]
+        me, xt, o, dy_stack, flat_out, flat_gu, flat_down, gain_all[1]
     )
-    output = swap(out_stack.reshape(slices * seqs, span, D))
-    packed = jnp.concatenate(
-        [g_out.reshape(world, -1), g_gu.reshape(world, -1), g_down.reshape(world, -1)], axis=1
-    )
-    owned = scatter_sum(packed)
-    gin_stack, g_qkv, gg1 = attention_backward(
-        me, xt, qkv, do, lse, delta, dr, mat_qkv, gain_all[0], cos, sin, slices
-    )
-    grad_input = swap(gin_stack.reshape(slices * seqs, span, D))
-    gg = jnp.concatenate([jnp.sum(gg1, axis=1), jnp.sum(gg2, axis=1)]).astype(BF)
+    output = place(me, give_back([out_stack[k] for k in range(slices)])).reshape(tokens.shape)
+    own_gu = reduce_terms(shares(g_gu), "xy")
+    own_down = reduce_terms(shares(g_down), "yx")
+    own_out = reduce_terms(shares(g_out), "yx")
+    back = [
+        attention_backward(s, me, xt, qkv, do, lse, delta, dr, mat_qkv, gain_all[0], cos, sin, slices)
+        for s in range(seqs)
+    ]
+    returned = [give_back([b[0][k] for k in range(slices)]) for b in back]
+    grad_input = jnp.concatenate([place(me, parts) for parts in returned], axis=1).reshape(tokens.shape)
+    g_qkv = sum(b[1] for b in back)
+    gg = jnp.concatenate([jnp.sum(sum(b[2] for b in back), axis=1), jnp.sum(gg2, axis=1)])
     late = jnp.concatenate([g_qkv.reshape(world, -1), gg.reshape(world, -1)], axis=1)
-    owned_late = scatter_sum(late)
-    n_qkv = w_qkv.shape[0]
+    own_late = reduce_terms(shares(late), "xy")
     return (
         output,
         grad_input,
-        owned_late[:n_qkv].astype(F32),
-        owned[:c1].astype(F32),
-        owned[c1:c2].astype(F32),
-        owned[c2 : c2 + w_down.shape[0]].astype(F32),
-        owned_late[n_qkv : n_qkv + gains.shape[0]].astype(F32),
+        own_late[:n_qkv],
+        own_out[: w_out.shape[0]],
+        own_gu[:c1],
+        own_down[: w_down.shape[0]],
+        own_late[n_qkv : n_qkv + n_gain],
     )
 
 

time: 729 us -> 666 us (0.914)
  waiting for transfers between devices: 371 us -> 111 us
  Pallas kernels: 184 us -> 369 us
  blocking collectives: 36 us -> 0 us
  starting transfers between devices: 12.8 us -> 48 us
  other arithmetic: 18.8 us -> 31.2 us
    unnamed x6 -> x1, waiting for transfers between devices: 168 us -> 0.02 us
    pallas_call x1 -> x4, Pallas kernels: 42.1 us -> 203 us  [the longest x3 162 us: place(): pl.pallas_call(place_kernel, grid_spec=pltpu.PrefetchScalarGridSpec(num_s...]
    reduce_scatter x1 -> x0, waiting for transfers between devices: 144 us -> none  [scatter_sum(): lax.psum_scatter(terms.reshape(world, -1, 128), both, scatter_dimension=0...]
    ppermute x0 -> x45, waiting for transfers between devices: none -> 111 us  [partner(): lax.ppermute(array, name, [(i, i ^ bits) for i in range(lax.axis_size(nam...]
    ppermute x0 -> x45, starting transfers between devices: none -> 48 us  [partner(): lax.ppermute(array, name, [(i, i ^ bits) for i in range(lax.axis_size(nam...]
    all_to_all x1 -> x0, blocking collectives: 36 us -> none  [swap(): return lax.all_to_all(array, 'ctx', split_axis=0, concat_axis=0, tiled=True)]
    all_gather x1, waiting for transfers between devices: 34.9 us -> 0.01 us  [local(): lax.all_gather(jnp.concatenate([w_gate_up, w_down, w_out]), both, axis=0,...]
    reshape x11 -> x6, local copies, waits for them, and re-layouts: 42.3 us -> 13.6 us  [the longest x1 5.12 us: local(): flat_gu = rest[:, :c1].reshape(-1, 128)]
  transfers between devices with their start and end apart: 7 -> 46, of which waited for: 5 -> 17; matrix products, arithmetic and copies ran while one was open for 6% -> 13% of each run, Pallas kernels for 6% -> 31%
where the time goes in v2:
time: 666 us; the launch traced here: 661 us
  Pallas kernels  369 us (55%)
  waiting for transfers between devices  111 us (17%)
  local copies, waits for them, and re-layouts  86.2 us (13%)
  starting transfers between devices  48 us (7%)
  other arithmetic  31.2 us (5%)
  between operations  15 us (2%)
    pallas_call x3, Pallas kernels, place(): pl.pallas_call(place_kernel, grid_spec=pltpu.PrefetchScalarGridSpec(num_s...  162 us
    ppermute x45, waiting for transfers between devices, partner(): lax.ppermute(array, name, [(i, i ^ bits) for i in range(lax.axis_size(nam...  111 us
    pallas_call x1, Pallas kernels, middle(): pl.pallas_call(middle_kernel, grid_spec=pltpu.PrefetchScalarGridSpec(num_...  90.4 us
    pallas_call x2, Pallas kernels, attention_backward(): pl.pallas_call(backward_kernel, grid_spec=pltpu.PrefetchScalarGridSpec(nu...  76 us
    ppermute x45, starting transfers between devices, partner(): lax.ppermute(array, name, [(i, i ^ bits) for i in range(lax.axis_size(nam...  48 us
    pallas_call x1, Pallas kernels, attention_forward(): pl.pallas_call(functools.partial(forward_kernel, slices), grid_spec=pltpu...  40.5 us
    unnamed x65, local copies, waits for them, and re-layouts  21.8 us
    ppermute x9, local copies, waits for them, and re-layouts, partner(): lax.ppermute(array, name, [(i, i ^ bits) for i in range(lax.axis_size(nam...  14.9 us
  transfers between devices with their start and end apart: 46, of which 17 were waited for; matrix products, arithmetic and copies ran while one was open for 13% of the time, Pallas kernels for 31%

profile of v2, /device:TPU:0, one launch (start us, length us, event | category | flops | bytes accessed | tf_op | source)
XLA Modules:
  0.0 660.7 jit_solution(17925636711790789093)
XLA Ops:
  9.9 3.0 collective-permute-start.3
  12.9 3.1 copy.77
  16.7 3.6 collective-permute-start.4
  22.5 2.3 copy.78
  32.3 2.8 dynamic-slice_bitcast_fusion.1
  35.1 2.1 collective-permute-start
  40.0 12.0 %collective-permute-done.10 = bf16[2,256,576]{1,2,0:T(8,128)(2,1)} collective-permute-done((bf16[2,256,576]{1,2,0:T(8,128)(2,1)}, bf16[2,256,576]{1,2,0:T(8,128)(2,1)}, u32[]{:S(2)}, u32[]{:S(2)}) %collective-permute-start.10) | collective-permute-done | bytes 589856 | tf_op jit(solution)/shard_map/ppermute | solution.py:521
  54.6 2.2 copy.81
  56.8 6.5 collective-permute-done.11
  63.3 2.1 copy.83
  66.8 19.0 %collective-permute-done.1 = bf16[2,256,576]{1,2,0:T(8,128)(2,1)} collective-permute-done((bf16[2,256,576]{1,2,0:T(8,128)(2,1)}, bf16[2,256,576]{1,2,0:T(8,128)(2,1)}, u32[]{:S(2)}, u32[]{:S(2)}) %collective-permute-start.1) | collective-permute-done | bytes 589856 | tf_op jit(solution)/shard_map/ppermute | solution.py:521
  87.2 18.4 %collective-permute-done.2 = bf16[2,256,576]{1,2,0:T(8,128)(2,1)} collective-permute-done((bf16[2,256,576]{1,2,0:T(8,128)(2,1)}, bf16[2,256,576]{1,2,0:T(8,128)(2,1)}, u32[]{:S(2)}, u32[]{:S(2)}) %collective-permute-start.2) | collective-permute-done | bytes 589856 | tf_op jit(solution)/shard_map/ppermute | solution.py:521
  105.6 2.2 copy.74.refs_3_
  107.8 3.3 pad_maximum_fusion.dy_ref
  113.3 2.7 maximum_bitcast_fusion
  116.1 2.1 copy.71
  121.0 3.1 reshape.150.w_ref
  124.1 2.1 copy.75.refs_4_
  130.8 40.5 %attention_forward.1 = (bf16[2,576,1024]{2,1,0:T(8,128)(2,1)}, bf16[2,960,1024]{2,1,0:T(8,128)(2,1)}, bf16[2,576,1024]{2,1,0:T(8,128)(2,1)}, f32[2,9,1024]{2,1,0:T(8,128)S(1)}) custom-call(s32[1]{0:T(128)} %bitcast.me_ref, bf16[2,256,576]{2,1,0:T(8,128)(2,1)S(1)} %bitcast.187, bf16[2,256,576]{2,1,0:T(8,128)(2,1)S(1)} %copy.72.refs_1_, ...), custom_call_target="tpu_custom_call" | custom-call | flops 9512681472 | bytes 14336000 | tf_op jit(solution)/shard_map/attention_forward/pallas_call | solution.py:381
  172.0 5.0 copy.99
  177.0 2.0 slice.96
  180.1 5.1 reshape.153.fgu_ref
  188.9 90.4 %middle.1 = (bf16[4,2,256,576]{3,2,1,0:T(8,128)(2,1)}, f32[2,576,1024]{2,1,0:T(8,128)}, bf16[2,576,1024]{2,1,0:T(8,128)(2,1)}, f32[2,9,1024]{2,1,0:T(8,128)}, f3...) custom-call(s32[1]{0:T(128)} %bitcast.me_ref, ...), custom_call_target="tpu_custom_call" | custom-call | flops 36691771392 | bytes 28384000 | tf_op jit(solution)/shard_map/middle/pallas_call | solution.py:414
  279.3 42.3 %attention_backward.2 = (bf16[4,1,256,576]{3,2,1,0:T(8,128)(2,1)}, f32[4320,128]{1,0:T(8,128)}, f32[576,128]{1,0:T(8,128)}) custom-call(s32[1]{0:T(128)} %bitcast.me_ref, bf16[2,576,1024]{2,1,0:T(8,128)(2,1)} %get-tuple-element.25.xt_ref, bf16[2,960,1024]{2,1,0:T(8,128)(2,1)} %get-tuple-element.28.qkv_ref, bf16[2,576,1024]{2,1,0:T(8,128)(2,1)} %get-tuple-element.29.do_ref, ...), custom_call_target="tpu_custom_call" | custom-call | flops 8304721920 | bytes 9216000 | tf_op jit(solution)/shard_map/attention_backward/pallas_call | solution.py:457
  321.6 33.7 %attention_backward.3 = (bf16[4,1,256,576]{3,2,1,0:T(8,128)(2,1)}, f32[4320,128]{1,0:T(8,128)}, f32[576,128]{1,0:T(8,128)}) custom-call(s32[1]{0:T(128)} %bitcast.me_ref, bf16[2,576,1024]{2,1,0:T(8,128)(2,1)} %get-tuple-element.25.xt_ref, bf16[2,960,1024]{2,1,0:T(8,128)(2,1)} %get-tuple-element.28.qkv_ref, bf16[2,576,1024]{2,1,0:T(8,128)(2,1)} %get-tuple-element.29.do_ref, ...), custom_call_target="tpu_custom_call" | custom-call | flops 8304721920 | bytes 9216000 | tf_op jit(solution)/shard_map/attention_backward/pallas_call | solution.py:457
  355.4 4.0 fusion.5
  359.5 2.5 collective-permute-start.27
  362.3 2.5 add.216
  376.8 4.4 collective-permute-done.16.refs_2_
  382.2 5.2 collective-permute-done.17.refs_3_
  392.9 40.8 %place.4 = bf16[4,1,256,576]{3,2,1,0:T(8,128)(2,1)} custom-call(s32[1]{0:T(128)} %bitcast.me_ref, bf16[1,256,576]{2,1,0:T(8,128)(2,1)} %get-tuple-element.93.refs_0_, bf16[1,256,576]{2,1,0:T(8,128)(2,1)} %copy-done.21, bf16[1,256,576]{2,1,0:T(8,128)(2,1)} %copy-done.22, bf16[1,256,576]{2,1,0:T(8,128)(2,1)} %copy-done.23), custom_call_target="tpu_custom_call" | custom-call | bytes 2359296 | tf_op jit(solution)/shard_map/place/pallas_call | solution.py:505
  434.5 40.8 %place.5 = bf16[4,1,256,576]{3,2,1,0:T(8,128)(2,1)} custom-call(s32[1]{0:T(128)} %bitcast.me_ref, bf16[1,256,576]{2,1,0:T(8,128)(2,1)} %get-tuple-element.97.refs_0_, bf16[1,256,576]{2,1,0:T(8,128)(2,1)} %collective-permute-done.18.refs_1_, bf16[1,256,576]{2,1,0:T(8,128)(2,1)} %collective-permute-done.19.refs_2_, ...), custom_call_target="tpu_custom_call" | custom-call | bytes 2359296 | tf_op jit(solution)/shard_map/place/pallas_call | solution.py:505
  477.1 2.1 pad_maximum_fusion.1
  479.1 2.8 copy.94
  488.0 2.1 copy.88.refs_1_
  490.1 8.2 %collective-permute-done.13 = bf16[2,256,576]{1,2,0:T(8,128)(2,1)S(1)} collective-permute-done((bf16[2,256,576]{1,2,0:T(8,128)(2,1)}, bf16[2,256,576]{1,2,0:T(8,128)(2,1)S(1)}, u32[]{:S(2)}, u32[]{:S(2)}) %collective-permute-start.13) | collective-permute-done | bytes 589856 | tf_op jit(solution)/shard_map/ppermute | solution.py:521
  500.7 9.1 %collective-permute-done.14 = bf16[2,256,576]{1,2,0:T(8,128)(2,1)S(1)} collective-permute-done((bf16[2,256,576]{1,2,0:T(8,128)(2,1)}, bf16[2,256,576]{1,2,0:T(8,128)(2,1)S(1)}, u32[]{:S(2)}, u32[]{:S(2)}) %collective-permute-start.14) | collective-permute-done | bytes 589856 | tf_op jit(solution)/shard_map/ppermute | solution.py:521
  511.0 80.5 %place.3 = bf16[4,2,256,576]{3,2,1,0:T(8,128)(2,1)} custom-call(s32[1]{0:T(128)} %bitcast.me_ref, bf16[2,256,576]{2,1,0:T(8,128)(2,1)} %get-tuple-element.81.refs_0_, bf16[2,256,576]{2,1,0:T(8,128)(2,1)} %copy.88.refs_1_, bf16[2,256,576]{2,1,0:T(8,128)(2,1)} %copy.89.refs_2_, bf16[2,256,576]{2,1,0:T(8,128)(2,1)} %copy.90.refs_3_), custom_call_target="tpu_custom_call" | custom-call | bytes 4718592 | tf_op jit(solution)/shard_map/place/pallas_call | solution.py:505
  591.5 4.3 copy.93
  595.9 3.6 collective-permute-start.32
  601.9 3.1 collective-permute-done.23
  606.0 2.9 fusion
  610.2 2.8 collective-permute-start.26
  616.2 2.2 collective-permute-start.41
  618.5 16.6 %collective-permute-done.34 = bf16[4,2,432,128]{3,2,1,0:T(8,128)(2,1)S(1)} collective-permute-done((bf16[4,2,432,128]{3,2,1,0:T(8,128)(2,1)S(1)}, bf16[4,2,432,128]{3,2,1,0:T(8,128)(2,1)S(1)}, u32[]{:S(2)}, u32[]{:S(2)}) %collective-permute-start.34) | collective-permute-done | bytes 884768 | tf_op jit(solution)/shard_map/ppermute | solution.py:521
  640.3 2.6 collective-permute-start.44
  645.8 2.6 collective-permute-start.38
  649.0 3.9 collective-permute-done.37
  (211 shorter events, 84.1 us)
Async XLA Ops:
  7.2 164.8 %all-gather.4.cloned.1.call-start = ((), (), s32[]{:S(2)}) async-start(), calls=%async_computation | async-start | bytes 12317184 | tf_op jit(solution)/shard_map/all_gather | solution.py:598
  9.9 6.1 collective-permute-start.3
  16.7 8.0 %collective-permute-start.4 = (bf16[2,136,128]{2,1,0:T(8,128)(2,1)}, bf16[2,136,128]{2,1,0:T(8,128)(2,1)S(1)}, u32[]{:S(2)}, u32[]{:S(2)}) collective-permute-start(bf16[2,136,128]{2,1,0:T(8,128)(2,1)} %pad_maximum_fusion.5), channel_id=1, source_target_pairs={{0,24},{4,28},{8,16},{12,20},{16,8},{20,12},{24,0},{28,4},{1,25},{... | collective-permute-start | bytes 208904 | tf_op jit(solution)/shard_map/ppermute | solution.py:521
  20.3 5.9 collective-permute-start.5
  20.3 7.3 %collective-permute-start.6 = (bf16[2,136,128]{2,1,0:T(8,128)(2,1)}, bf16[2,136,128]{2,1,0:T(8,128)(2,1)}, u32[]{:S(2)}, u32[]{:S(2)}) collective-permute-start(bf16[2,136,128]{2,1,0:T(8,128)(2,1)} %pad_maximum_fusion.5), channel_id=1, source_target_pairs={{0,8},{4,12},{8,0},{12,4},{16,24},{20,28},{24,16},{28,20},{1,9},{5... | collective-permute-start | bytes 208904 | tf_op jit(solution)/shard_map/ppermute | solution.py:521
  24.8 13.0 %collective-permute-start.9 = (bf16[2,256,576]{1,2,0:T(8,128)(2,1)}, bf16[2,256,576]{1,2,0:T(8,128)(2,1)S(1)}, u32[]{:S(2)}, u32[]{:S(2)}) collective-permute-start(bf16[2,256,576]{1,2,0:T(8,128)(2,1)} %bitcast.205), channel_id=1, source_target_pairs={{0,1},{1,0},{2,3},{3,2},{4,5},{5,4},{6,7},{7,6},{8,9},{9,8},{10,11... | collective-permute-start | bytes 1769480 | tf_op jit(solution)/shard_map/ppermute | solution.py:521
  28.6 9.0 %collective-permute-start.7 = (bf16[4,2,136,128]{3,2,1,0:T(8,128)(2,1)S(1)}, bf16[4,2,136,128]{3,2,1,0:T(8,128)(2,1)S(1)}, u32[]{:S(2)}, u32[]{:S(2)}) collective-permute-start(bf16[4,2,136,128]{3,2,1,0:T(8,128)(2,1)S(1)} %pad_maximum_fusion.3), channel_id=1, source_target_pairs={{0,4},{4,0},{8,12},{12,8},{16,20},{20,16},{24,28},{28,24},{1,5},{5... | collective-permute-start | bytes 835592 | tf_op jit(solution)/shard_map/ppermute | solution.py:521
  31.2 20.8 %collective-permute-start.10 = (bf16[2,256,576]{1,2,0:T(8,128)(2,1)}, bf16[2,256,576]{1,2,0:T(8,128)(2,1)}, u32[]{:S(2)}, u32[]{:S(2)}) collective-permute-start(bf16[2,256,576]{1,2,0:T(8,128)(2,1)} %bitcast.206), channel_id=1, source_target_pairs={{0,2},{1,3},{2,0},{3,1},{4,6},{5,7},{6,4},{7,5},{8,10},{9,11},{10,... | collective-permute-start | bytes 1769480 | tf_op jit(solution)/shard_map/ppermute | solution.py:521
  32.3 31.0 %collective-permute-start.11 = (bf16[2,256,576]{1,2,0:T(8,128)(2,1)}, bf16[2,256,576]{1,2,0:T(8,128)(2,1)}, u32[]{:S(2)}, u32[]{:S(2)}) collective-permute-start(bf16[2,256,576]{1,2,0:T(8,128)(2,1)} %bitcast.22), channel_id=1, source_target_pairs={{0,3},{1,2},{2,1},{3,0},{4,7},{5,6},{6,5},{7,4},{8,11},{9,10},{10,... | collective-permute-start | bytes 1769480 | tf_op jit(solution)/shard_map/ppermute | solution.py:521
  35.1 30.3 %collective-permute-start = (bf16[2,256,576]{1,2,0:T(8,128)(2,1)}, bf16[2,256,576]{1,2,0:T(8,128)(2,1)}, u32[]{:S(2)}, u32[]{:S(2)}) collective-permute-start(bf16[2,256,576]{1,2,0:T(8,128)(2,1)} %get-tuple-element.88), channel_id=1, source_target_pairs={{0,1},{1,0},{2,3},{3,2},{4,5},{5,4},{6,7},{7,6},{8,9},{9,8},{10,11... | collective-permute-start | bytes 1769480 | tf_op jit(solution)/shard_map/ppermute | solution.py:521
  37.6 48.2 %collective-permute-start.1 = (bf16[2,256,576]{1,2,0:T(8,128)(2,1)}, bf16[2,256,576]{1,2,0:T(8,128)(2,1)}, u32[]{:S(2)}, u32[]{:S(2)}) collective-permute-start(bf16[2,256,576]{1,2,0:T(8,128)(2,1)} %get-tuple-element.87), channel_id=1, source_target_pairs={{0,2},{1,3},{2,0},{3,1},{4,6},{5,7},{6,4},{7,5},{8,10},{9,11},{10,... | collective-permute-start | bytes 1769480 | tf_op jit(solution)/shard_map/ppermute | solution.py:521
  37.7 67.8 %collective-permute-start.2 = (bf16[2,256,576]{1,2,0:T(8,128)(2,1)}, bf16[2,256,576]{1,2,0:T(8,128)(2,1)}, u32[]{:S(2)}, u32[]{:S(2)}) collective-permute-start(bf16[2,256,576]{1,2,0:T(8,128)(2,1)} %get-tuple-element.86), channel_id=1, source_target_pairs={{0,3},{1,2},{2,1},{3,0},{4,7},{5,6},{6,5},{7,4},{8,11},{9,10},{10,... | collective-permute-start | bytes 1769480 | tf_op jit(solution)/shard_map/ppermute | solution.py:521
  52.0 59.1 %collective-permute-start.8 = (bf16[2,4,2,136,128]{4,3,2,1,0:T(8,128)(2,1)}, bf16[2,4,2,136,128]{4,3,2,1,0:T(8,128)(2,1)}, u32[]{:S(2)}, u32[]{:S(2)}) collective-permute-start(bf16[2,4,2,136,128]{4,3,2,1,0:T(8,128)(2,1)} %pad_maximum_fusion.2), channel_id=1, source_target_pairs={{0,1},{1,0},{2,3},{3,2},{4,5},{5,4},{6,7},{7,6},{8,9},{9,8},{10,11... | collective-permute-start | bytes 1671176 | tf_op jit(solution)/shard_map/ppermute | solution.py:521
  127.1 44.3 %copy-start.1 = (f32[576,1]{1,0:T(8,128)}, f32[576,1]{1,0:T(8,128)S(1)}, u32[]{:S(2)}) copy-start(f32[576,1]{1,0:T(8,128)S(1)} %squeeze.216.refs_5_.gain_ref) | copy-start | bytes 6916
  321.6 33.7 %copy-start.15 = (f32[2592,128]{1,0:T(8,128)S(1)}, f32[2592,128]{1,0:T(8,128)}, u32[]{:S(2)}) copy-start(f32[2592,128]{1,0:T(8,128)} %get-tuple-element.40) | copy-start | bytes 3981316
  359.5 15.6 %collective-permute-start.27 = (bf16[4,2,2,81,128]{4,3,2,1,0:T(8,128)(2,1)S(1)}, bf16[4,2,2,81,128]{4,3,2,1,0:T(8,128)(2,1)S(1)}, u32[]{:S(2)}, u32[]{:S(2)}) collective-permute-start(bf16[4,2,2,81,128]{4,3,2,1,0:T(8,128)(2,1)S(1)} %fusion.16), channel_id=1, source_target_pairs={{0,1},{1,0},{2,3},{3,2},{4,5},{5,4},{6,7},{7,6},{8,9},{9,8},{10,11... | collective-permute-start | bytes 995336 | tf_op jit(solution)/shard_map/ppermute | solution.py:521
  370.7 4.9 collective-permute-start.15
  370.7 10.5 %collective-permute-start.16 = (bf16[1,256,576]{2,1,0:T(8,128)(2,1)S(1)}, bf16[1,256,576]{2,1,0:T(8,128)(2,1)S(1)}, u32[]{:S(2)}, u32[]{:S(2)}) collective-permute-start(bf16[1,256,576]{2,1,0:T(8,128)(2,1)S(1)} %get-tuple-element.91), channel_id=1, source_target_pairs={{0,2},{1,3},{2,0},{3,1},{4,6},{5,7},{6,4},{7,5},{8,10},{9,11},{10,... | collective-permute-start | bytes 884744 | tf_op jit(solution)/shard_map/ppermute | solution.py:521
  370.8 16.7 %collective-permute-start.17 = (bf16[1,256,576]{2,1,0:T(8,128)(2,1)S(1)}, bf16[1,256,576]{2,1,0:T(8,128)(2,1)S(1)}, u32[]{:S(2)}, u32[]{:S(2)}) collective-permute-start(bf16[1,256,576]{2,1,0:T(8,128)(2,1)S(1)} %get-tuple-element.90), channel_id=1, source_target_pairs={{0,3},{1,2},{2,1},{3,0},{4,7},{5,6},{6,5},{7,4},{8,11},{9,10},{10,... | collective-permute-start | bytes 884744 | tf_op jit(solution)/shard_map/ppermute | solution.py:521
  373.6 60.1 %collective-permute-start.18 = (bf16[1,256,576]{2,1,0:T(8,128)(2,1)}, bf16[1,256,576]{2,1,0:T(8,128)(2,1)}, u32[]{:S(2)}, u32[]{:S(2)}) collective-permute-start(bf16[1,256,576]{2,1,0:T(8,128)(2,1)} %get-tuple-element.96), channel_id=1, source_target_pairs={{0,1},{1,0},{2,3},{3,2},{4,5},{5,4},{6,7},{7,6},{8,9},{9,8},{10,11... | collective-permute-start | bytes 884744 | tf_op jit(solution)/shard_map/ppermute | solution.py:521
  375.1 58.9 %collective-permute-start.19 = (bf16[1,256,576]{2,1,0:T(8,128)(2,1)}, bf16[1,256,576]{2,1,0:T(8,128)(2,1)}, u32[]{:S(2)}, u32[]{:S(2)}) collective-permute-start(bf16[1,256,576]{2,1,0:T(8,128)(2,1)} %get-tuple-element.95), channel_id=1, source_target_pairs={{0,2},{1,3},{2,0},{3,1},{4,6},{5,7},{6,4},{7,5},{8,10},{9,11},{10,... | collective-permute-start | bytes 884744 | tf_op jit(solution)/shard_map/ppermute | solution.py:521
  375.7 58.7 %collective-permute-start.20 = (bf16[1,256,576]{2,1,0:T(8,128)(2,1)}, bf16[1,256,576]{2,1,0:T(8,128)(2,1)}, u32[]{:S(2)}, u32[]{:S(2)}) collective-permute-start(bf16[1,256,576]{2,1,0:T(8,128)(2,1)} %get-tuple-element.94), channel_id=1, source_target_pairs={{0,3},{1,2},{2,1},{3,0},{4,7},{5,6},{6,5},{7,4},{8,11},{9,10},{10,... | collective-permute-start | bytes 884744 | tf_op jit(solution)/shard_map/ppermute | solution.py:521
  381.2 94.1 %collective-permute-start.28 = (bf16[4,2,81,128]{3,2,1,0:T(8,128)(2,1)S(1)}, bf16[4,2,81,128]{3,2,1,0:T(8,128)(2,1)}, u32[]{:S(2)}, u32[]{:S(2)}) collective-permute-start(bf16[4,2,81,128]{3,2,1,0:T(8,128)(2,1)S(1)} %dynamic-slice_bitcast_fusion.8), channel_id=1, source_target_pairs={{0,2},{1,3},{2,0},{3,1},{4,6},{5,7},{6,4},{7,5},{8,10},{9,11},{10,... | collective-permute-start | bytes 497672 | tf_op jit(solution)/shard_map/ppermute | solution.py:521
  387.4 94.5 %collective-permute-start.21 = (bf16[4,2,2,136,128]{4,3,2,1,0:T(8,128)(2,1)}, bf16[4,2,2,136,128]{4,3,2,1,0:T(8,128)(2,1)}, u32[]{:S(2)}, u32[]{:S(2)}) collective-permute-start(bf16[4,2,2,136,128]{4,3,2,1,0:T(8,128)(2,1)} %fusion.13), channel_id=1, source_target_pairs={{0,1},{1,0},{2,3},{3,2},{4,5},{5,4},{6,7},{7,6},{8,9},{9,8},{10,11... | collective-permute-start | bytes 1671176 | tf_op jit(solution)/shard_map/ppermute | solution.py:521
  433.8 165.8 %collective-permute-start.39 = (bf16[4,2,2,216,128]{4,3,2,1,0:T(8,128)(2,1)S(1)}, bf16[4,2,2,216,128]{4,3,2,1,0:T(8,128)(2,1)}, u32[]{:S(2)}, u32[]{:S(2)}) collective-permute-start(bf16[4,2,2,216,128]{4,3,2,1,0:T(8,128)(2,1)S(1)} %fusion.9), channel_id=1, source_target_pairs={{0,1},{1,0},{2,3},{3,2},{4,5},{5,4},{6,7},{7,6},{8,9},{9,8},{10,11... | collective-permute-start | bytes 2654216 | tf_op jit(solution)/shard_map/ppermute | solution.py:521
  434.0 171.5 %collective-permute-start.33 = (bf16[4,2,2,432,128]{4,3,2,1,0:T(8,128)(2,1)}, bf16[4,2,2,432,128]{4,3,2,1,0:T(8,128)(2,1)}, u32[]{:S(2)}, u32[]{:S(2)}) collective-permute-start(bf16[4,2,2,432,128]{4,3,2,1,0:T(8,128)(2,1)} %fusion.5), channel_id=1, source_target_pairs={{0,1},{1,0},{2,3},{3,2},{4,5},{5,4},{6,7},{7,6},{8,9},{9,8},{10,11... | collective-permute-start | bytes 5308424 | tf_op jit(solution)/shard_map/ppermute | solution.py:521
  434.4 50.8 %collective-permute-start.12 = (bf16[2,256,576]{1,2,0:T(8,128)(2,1)}, bf16[2,256,576]{1,2,0:T(8,128)(2,1)}, u32[]{:S(2)}, u32[]{:S(2)}) collective-permute-start(bf16[2,256,576]{1,2,0:T(8,128)(2,1)} %copy.85), channel_id=1, source_target_pairs={{0,1},{1,0},{2,3},{3,2},{4,5},{5,4},{6,7},{7,6},{8,9},{9,8},{10,11... | collective-permute-start | bytes 1769480 | tf_op jit(solution)/shard_map/ppermute | solution.py:521
  477.0 5.2 collective-permute-start.29
  481.9 16.4 %collective-permute-start.13 = (bf16[2,256,576]{1,2,0:T(8,128)(2,1)}, bf16[2,256,576]{1,2,0:T(8,128)(2,1)S(1)}, u32[]{:S(2)}, u32[]{:S(2)}) collective-permute-start(bf16[2,256,576]{1,2,0:T(8,128)(2,1)} %copy.86), channel_id=1, source_target_pairs={{0,2},{1,3},{2,0},{3,1},{4,6},{5,7},{6,4},{7,5},{8,10},{9,11},{10,... | collective-permute-start | bytes 1769480 | tf_op jit(solution)/shard_map/ppermute | solution.py:521
  482.3 27.5 %collective-permute-start.14 = (bf16[2,256,576]{1,2,0:T(8,128)(2,1)}, bf16[2,256,576]{1,2,0:T(8,128)(2,1)S(1)}, u32[]{:S(2)}, u32[]{:S(2)}) collective-permute-start(bf16[2,256,576]{1,2,0:T(8,128)(2,1)} %copy.87), channel_id=1, source_target_pairs={{0,3},{1,2},{2,1},{3,0},{4,7},{5,6},{6,5},{7,4},{8,11},{9,10},{10,... | collective-permute-start | bytes 1769480 | tf_op jit(solution)/shard_map/ppermute | solution.py:521
  485.2 110.7 %collective-permute-start.22 = (bf16[4,2,136,128]{3,2,1,0:T(8,128)(2,1)S(1)}, bf16[4,2,136,128]{3,2,1,0:T(8,128)(2,1)S(1)}, u32[]{:S(2)}, u32[]{:S(2)}) collective-permute-start(bf16[4,2,136,128]{3,2,1,0:T(8,128)(2,1)S(1)} %dynamic-slice_bitcast_fusion.6), channel_id=1, source_target_pairs={{0,4},{4,0},{8,12},{12,8},{16,20},{20,16},{24,28},{28,24},{1,5},{5... | collective-permute-start | bytes 835592 | tf_op jit(solution)/shard_map/ppermute | solution.py:521
  498.3 110.6 %collective-permute-start.30 = (bf16[81,128]{1,0:T(8,128)(2,1)S(1)}, bf16[81,128]{1,0:T(8,128)(2,1)S(1)}, u32[]{:S(2)}, u32[]{:S(2)}) collective-permute-start(bf16[81,128]{1,0:T(8,128)(2,1)S(1)} %get-tuple-element.115), channel_id=1, source_target_pairs={{0,8},{4,12},{8,0},{12,4},{16,24},{20,28},{24,16},{28,20},{1,9},{5... | collective-permute-start | bytes 62216 | tf_op jit(solution)/shard_map/ppermute | solution.py:521
  509.8 100.4 %collective-permute-start.31 = (bf16[81,128]{1,0:T(8,128)(2,1)S(1)}, bf16[81,128]{1,0:T(8,128)(2,1)S(1)}, u32[]{:S(2)}, u32[]{:S(2)}) collective-permute-start(bf16[81,128]{1,0:T(8,128)(2,1)S(1)} %get-tuple-element.117), channel_id=1, source_target_pairs={{0,16},{4,20},{8,24},{12,28},{16,0},{20,4},{24,8},{28,12},{1,17},{... | collective-permute-start | bytes 62216 | tf_op jit(solution)/shard_map/ppermute | solution.py:521
  595.9 17.1 %collective-permute-start.32 = (bf16[81,128]{1,0:T(8,128)(2,1)S(1)}, bf16[81,128]{1,0:T(8,128)(2,1)S(1)}, u32[]{:S(2)}, u32[]{:S(2)}) collective-permute-start(bf16[81,128]{1,0:T(8,128)(2,1)S(1)} %get-tuple-element.116), channel_id=1, source_target_pairs={{0,24},{4,28},{8,16},{12,20},{16,8},{20,12},{24,0},{28,4},{1,25},{... | collective-permute-start | bytes 62216 | tf_op jit(solution)/shard_map/ppermute | solution.py:521
  599.6 5.4 collective-permute-start.23
  605.1 11.0 %collective-permute-start.40 = (bf16[4,2,216,128]{3,2,1,0:T(8,128)(2,1)S(1)}, bf16[4,2,216,128]{3,2,1,0:T(8,128)(2,1)S(1)}, u32[]{:S(2)}, u32[]{:S(2)}) collective-permute-start(bf16[4,2,216,128]{3,2,1,0:T(8,128)(2,1)S(1)} %dynamic-slice_bitcast_fusion.4), channel_id=1, source_target_pairs={{0,2},{1,3},{2,0},{3,1},{4,6},{5,7},{6,4},{7,5},{8,10},{9,11},{10,... | collective-permute-start | bytes 1327112 | tf_op jit(solution)/shard_map/ppermute | solution.py:521
  605.5 9.9 %collective-permute-start.24 = (bf16[136,128]{1,0:T(8,128)(2,1)S(1)}, bf16[136,128]{1,0:T(8,128)(2,1)S(1)}, u32[]{:S(2)}, u32[]{:S(2)}) collective-permute-start(bf16[136,128]{1,0:T(8,128)(2,1)S(1)} %get-tuple-element.112), channel_id=1, source_target_pairs={{0,8},{4,12},{8,0},{12,4},{16,24},{20,28},{24,16},{28,20},{1,9},{5... | collective-permute-start | bytes 104456 | tf_op jit(solution)/shard_map/ppermute | solution.py:521
  608.9 6.4 collective-permute-start.25
  610.2 5.8 collective-permute-start.26
  613.0 22.1 %collective-permute-start.34 = (bf16[4,2,432,128]{3,2,1,0:T(8,128)(2,1)S(1)}, bf16[4,2,432,128]{3,2,1,0:T(8,128)(2,1)S(1)}, u32[]{:S(2)}, u32[]{:S(2)}) collective-permute-start(bf16[4,2,432,128]{3,2,1,0:T(8,128)(2,1)S(1)} %dynamic-slice_bitcast_fusion), channel_id=1, source_target_pairs={{0,4},{4,0},{8,12},{12,8},{16,20},{20,16},{24,28},{28,24},{1,5},{5... | collective-permute-start | bytes 2654216 | tf_op jit(solution)/shard_map/ppermute | solution.py:521
  616.2 22.1 %collective-permute-start.41 = (bf16[4,216,128]{2,1,0:T(8,128)(2,1)S(1)}, bf16[4,216,128]{2,1,0:T(8,128)(2,1)S(1)}, u32[]{:S(2)}, u32[]{:S(2)}) collective-permute-start(bf16[4,216,128]{2,1,0:T(8,128)(2,1)S(1)} %dynamic-slice_bitcast_fusion.7), channel_id=1, source_target_pairs={{0,4},{4,0},{8,12},{12,8},{16,20},{20,16},{24,28},{28,24},{1,5},{5... | collective-permute-start | bytes 663560 | tf_op jit(solution)/shard_map/ppermute | solution.py:521
  635.4 8.4 %collective-permute-start.35 = (bf16[4,432,128]{2,1,0:T(8,128)(2,1)S(1)}, bf16[4,432,128]{2,1,0:T(8,128)(2,1)S(1)}, u32[]{:S(2)}, u32[]{:S(2)}) collective-permute-start(bf16[4,432,128]{2,1,0:T(8,128)(2,1)S(1)} %dynamic-slice_bitcast_fusion.5), channel_id=1, source_target_pairs={{0,2},{1,3},{2,0},{3,1},{4,6},{5,7},{6,4},{7,5},{8,10},{9,11},{10,... | collective-permute-start | bytes 1327112 | tf_op jit(solution)/shard_map/ppermute | solution.py:521
  638.4 7.4 %collective-permute-start.42 = (bf16[216,128]{1,0:T(8,128)(2,1)S(1)}, bf16[216,128]{1,0:T(8,128)(2,1)S(1)}, u32[]{:S(2)}, u32[]{:S(2)}) collective-permute-start(bf16[216,128]{1,0:T(8,128)(2,1)S(1)} %get-tuple-element.109), channel_id=1, source_target_pairs={{0,8},{4,12},{8,0},{12,4},{16,24},{20,28},{24,16},{28,20},{1,9},{5... | collective-permute-start | bytes 165896 | tf_op jit(solution)/shard_map/ppermute | solution.py:521
  638.5 9.9 %collective-permute-start.43 = (bf16[216,128]{1,0:T(8,128)(2,1)S(1)}, bf16[216,128]{1,0:T(8,128)(2,1)S(1)}, u32[]{:S(2)}, u32[]{:S(2)}) collective-permute-start(bf16[216,128]{1,0:T(8,128)(2,1)S(1)} %get-tuple-element.111), channel_id=1, source_target_pairs={{0,16},{4,20},{8,24},{12,28},{16,0},{20,4},{24,8},{28,12},{1,17},{... | collective-permute-start | bytes 165896 | tf_op jit(solution)/shard_map/ppermute | solution.py:521
  640.3 8.1 %collective-permute-start.44 = (bf16[216,128]{1,0:T(8,128)(2,1)S(1)}, bf16[216,128]{1,0:T(8,128)(2,1)S(1)}, u32[]{:S(2)}, u32[]{:S(2)}) collective-permute-start(bf16[216,128]{1,0:T(8,128)(2,1)S(1)} %get-tuple-element.110), channel_id=1, source_target_pairs={{0,24},{4,28},{8,16},{12,20},{16,8},{20,12},{24,0},{28,4},{1,25},{... | collective-permute-start | bytes 165896 | tf_op jit(solution)/shard_map/ppermute | solution.py:521
  643.9 5.1 collective-permute-start.36
  644.0 8.9 %collective-permute-start.37 = (bf16[432,128]{1,0:T(8,128)(2,1)S(1)}, bf16[432,128]{1,0:T(8,128)(2,1)S(1)}, u32[]{:S(2)}, u32[]{:S(2)}) collective-permute-start(bf16[432,128]{1,0:T(8,128)(2,1)S(1)} %get-tuple-element.104), channel_id=1, source_target_pairs={{0,16},{4,20},{8,24},{12,28},{16,0},{20,4},{24,8},{28,12},{1,17},{... | collective-permute-start | bytes 331784 | tf_op jit(solution)/shard_map/ppermute | solution.py:521
  645.8 7.1 %collective-permute-start.38 = (bf16[432,128]{1,0:T(8,128)(2,1)S(1)}, bf16[432,128]{1,0:T(8,128)(2,1)S(1)}, u32[]{:S(2)}, u32[]{:S(2)}) collective-permute-start(bf16[432,128]{1,0:T(8,128)(2,1)S(1)} %get-tuple-element.103), channel_id=1, source_target_pairs={{0,24},{4,28},{8,16},{12,20},{16,8},{20,12},{24,0},{28,4},{1,25},{... | collective-permute-start | bytes 331784 | tf_op jit(solution)/shard_map/ppermute | solution.py:521
  (27 other events, 148.3 us)
Sparse Core Ops, SparseCore 0:
  10.9 113.3 all-gather.3
